TPU v7x, 32 devices: a whole 2x2x4 slice. The times are simulated.
32 devices in a mesh: dp: 16 (over z, y, x), head: 2 (over core).
Axes of the slice: x: 2, y: 2, z: 4, core: 2. Of those that a mesh axis runs over, the one named last changes fastest.
Arguments:
- patches: bfloat16 [16384, 768], P('dp'), may hold values from -6 to 6
- image_grids: int32 [96, 2], P('dp'), may hold values from 0 to 24, as said below
- out_grad: bfloat16 [16384, 768], P('dp'), may hold values from -6 to 6
- first_gain: float32 [768], replicated, may hold values from 0.5 to 1.5
- first_shift: float32 [768], replicated, may hold values from -1 to 1
- qkv_weight: bfloat16 [3, 768, 768], P(None, None, 'head'), may hold values from -0.21875 to 0.21875
- qkv_bias: float32 [3, 768], P(None, 'head'), may hold values from -1 to 1
- rope_freqs: float32 [2, 12, 32], P(None, 'head'), may hold values from -0.8 to 0.8
- proj_weight: bfloat16 [768, 768], P('head'), may hold values from -2.5 to 2.5
- proj_bias: float32 [768], replicated, may hold values from -1 to 1
- second_gain: float32 [768], replicated, may hold values from 0.5 to 1.5
- second_shift: float32 [768], replicated, may hold values from -1 to 1
- expand_weight: bfloat16 [768, 3072], P(None, 'head'), may hold values from -0.21875 to 0.21875
- expand_bias: float32 [3072], P('head'), may hold values from -1 to 1
- contract_weight: bfloat16 [3072, 768], P('head'), may hold values from -0.109375 to 0.109375
- contract_bias: float32 [768], replicated, may hold values from -1 to 1
Outputs:
- mixed_out: bfloat16 [16384, 768], P('dp')
- patches_grad: float32 [16384, 768], P('dp')
- qkv_weight_grad: float32 [3, 768, 768], P(None, 'dp', 'head')
- proj_weight_grad: float32 [768, 768], P('head', 'dp')
- expand_weight_grad: float32 [768, 3072], P('dp', 'head')
- contract_weight_grad: float32 [3072, 768], P('head', 'dp')
- first_gain_grad: float32 [768], replicated
- first_shift_grad: float32 [768], replicated
- qkv_bias_grad: float32 [3, 768], P(None, 'head')
- rope_freqs_grad: float32 [2, 12, 32], P(None, 'head')
- proj_bias_grad: float32 [768], replicated
- second_gain_grad: float32 [768], replicated
- second_shift_grad: float32 [768], replicated
- expand_bias_grad: float32 [3072], P('head')
- contract_bias_grad: float32 [768], replicated
Inputs may be any that keep to these rules, and one draw needn't show every extreme that they name: `image_grids`: every image is square with side 14, 20 or 24, height equal to width. In each block of 6 rows (one index of dp) the images come first and the empty slots (0, 0) after them; the images' patches total at most 1024, and every block has an empty slot.
All inputs are finite; a program needn't handle non-finite values.
Results may differ from a plain program's by a relative error of at most 0.012.
Values sent between devices are 32-bit elements; how exact they have to be, the bound alone decides.
A program may use at most 192 MiB of HBM per device.

v0:
```python
from functools import partial

import jax
import jax.numpy as jnp
from jax import lax
from jax.sharding import PartitionSpec as P

eps = 1e-06
masked_score = -1e30


def positions(image_grids, row_count):
    slot_count = image_grids.shape[0]
    image_len = image_grids[:, 0] * image_grids[:, 1]
    image_end = jnp.cumsum(image_len)
    image_start = image_end - image_len
    token_pos = jnp.arange(row_count, dtype=jnp.int32)
    segment = jnp.sum((token_pos[:, None] >= image_end[None, :]).astype(jnp.int32), axis=1)
    member = segment[:, None] == jnp.arange(slot_count, dtype=jnp.int32)[None, :]
    start_tok = jnp.sum(jnp.where(member, image_start[None, :], 0), axis=1)
    width_tok = jnp.sum(jnp.where(member, image_grids[None, :, 1], 0), axis=1)
    offset = token_pos - start_tok
    safe_width = jnp.maximum(width_tok, 1)
    real_row = segment < slot_count
    grid_row = jnp.where(real_row, offset // safe_width, 0).astype(jnp.float32)
    grid_col = jnp.where(real_row, offset % safe_width, 0).astype(jnp.float32)
    return (segment, grid_row, grid_col, real_row.astype(jnp.float32))


def layer_norm_parts(source, gain, shift):
    mean_val = jnp.mean(source, axis=-1, keepdims=True)
    centred = source - mean_val
    inv_dev = lax.rsqrt(jnp.mean(centred * centred, axis=-1, keepdims=True) + eps)
    unit = centred * inv_dev
    return (unit * gain + shift, unit, inv_dev)


def norm_back(upstream, unit, inv_dev, gain):
    scaled = upstream * gain
    return inv_dev * (
        scaled
        - jnp.mean(scaled, axis=-1, keepdims=True)
        - unit * jnp.mean(scaled * unit, axis=-1, keepdims=True)
    )


def rotate_pairs(source, cosine, sine_val):
    row_count = source.shape[0]
    head_count = cosine.shape[1]
    half_size = cosine.shape[2]
    shaped = source.reshape(row_count, head_count, 2, half_size)
    first_half = shaped[:, :, 0]
    second_half = shaped[:, :, 1]
    turned = jnp.stack(
        [
            first_half * cosine - second_half * sine_val,
            first_half * sine_val + second_half * cosine,
        ],
        axis=2,
    )
    return turned.reshape(row_count, head_count * 2 * half_size)


def rotate_back(grad_rot, turned, cosine, sine_val):
    row_count = grad_rot.shape[0]
    head_count = cosine.shape[1]
    half_size = cosine.shape[2]
    grad_shaped = grad_rot.reshape(row_count, head_count, 2, half_size)
    turn_shaped = turned.reshape(row_count, head_count, 2, half_size)
    grad_first = grad_shaped[:, :, 0]
    grad_second = grad_shaped[:, :, 1]
    input_grad = jnp.stack(
        [
            grad_first * cosine + grad_second * sine_val,
            grad_second * cosine - grad_first * sine_val,
        ],
        axis=2,
    )
    angle_grad = grad_second * turn_shaped[:, :, 0] - grad_first * turn_shaped[:, :, 1]
    return (input_grad.reshape(row_count, head_count * 2 * half_size), angle_grad)


def attend_forward(query_low, key_low, value_low, segment, head_count):
    row_count = query_low.shape[0]
    head_size = query_low.shape[1] // head_count
    block = min(512, row_count)
    count = row_count // block
    score_scale = head_size ** (-0.5)
    key_heads = key_low.reshape(row_count, head_count, head_size)
    value_heads = value_low.reshape(row_count, head_count, head_size)
    query_blocks = query_low.reshape(count, block, head_count, head_size)
    segment_blocks = segment.reshape(count, block)

    def one_block(block_item):
        query_block, segment_query = block_item
        scores = (
            jnp.einsum("qhd,khd->hqk", query_block, key_heads, preferred_element_type=jnp.float32)
            * score_scale
        )
        same_image = (segment_query[:, None] == segment[None, :])[None]
        scores = jnp.where(same_image, scores, masked_score)
        row_max = jnp.max(scores, axis=-1, keepdims=True)
        exp_scores = jnp.exp(scores - row_max)
        row_total = jnp.sum(exp_scores, axis=-1, keepdims=True)
        probabilities = (exp_scores / row_total).astype(jnp.bfloat16)
        block_out = jnp.einsum(
            "hqk,khd->qhd", probabilities, value_heads, preferred_element_type=jnp.float32
        )
        return (block_out, (row_max + jnp.log(row_total))[..., 0])

    block_outs, log_sum = lax.map(one_block, (query_blocks, segment_blocks))
    return (block_outs.reshape(row_count, head_count * head_size), log_sum)


def attend_backward(query_low, key_low, value_low, attended_grad, log_sum, segment, head_count):
    row_count = query_low.shape[0]
    head_size = query_low.shape[1] // head_count
    block = min(512, row_count)
    count = row_count // block
    score_scale = head_size ** (-0.5)
    key_heads = key_low.reshape(row_count, head_count, head_size)
    value_heads = value_low.reshape(row_count, head_count, head_size)
    query_blocks = query_low.reshape(count, block, head_count, head_size)
    grad_blocks = attended_grad.reshape(count, block, head_count, head_size)
    segment_blocks = segment.reshape(count, block)

    def one_block(carry, block_item):
        key_grad, value_grad = carry
        query_block, grad_block, log_block, segment_query = block_item
        scores = (
            jnp.einsum("qhd,khd->hqk", query_block, key_heads, preferred_element_type=jnp.float32)
            * score_scale
        )
        same_image = (segment_query[:, None] == segment[None, :])[None]
        scores = jnp.where(same_image, scores, masked_score)
        probabilities = jnp.exp(scores - log_block[..., None])
        value_grad = value_grad + jnp.einsum(
            "hqk,qhd->khd",
            probabilities.astype(jnp.bfloat16),
            grad_block,
            preferred_element_type=jnp.float32,
        )
        prob_grad = jnp.einsum(
            "qhd,khd->hqk", grad_block, value_heads, preferred_element_type=jnp.float32
        )
        inner = jnp.sum(probabilities * prob_grad, axis=-1, keepdims=True)
        score_grad = (probabilities * (prob_grad - inner)).astype(jnp.bfloat16)
        query_grad = (
            jnp.einsum("hqk,khd->qhd", score_grad, key_heads, preferred_element_type=jnp.float32)
            * score_scale
        )
        key_grad = (
            key_grad
            + jnp.einsum(
                "hqk,qhd->khd", score_grad, query_block, preferred_element_type=jnp.float32
            )
            * score_scale
        )
        return ((key_grad, value_grad), query_grad)

    empty = jnp.zeros((row_count, head_count, head_size), jnp.float32)
    (key_grad, value_grad), query_grads = lax.scan(
        one_block, (empty, empty), (query_blocks, grad_blocks, log_sum, segment_blocks)
    )
    width = head_count * head_size
    return (
        query_grads.reshape(row_count, width),
        key_grad.reshape(row_count, width),
        value_grad.reshape(row_count, width),
    )


def run_forward(source, params, cosine, sine_val, segment):
    (
        gain_one,
        shift_one,
        weight_qkv,
        bias_qkv,
        weight_proj,
        bias_proj,
        gain_two,
        shift_two,
        weight_expand,
        bias_expand,
        weight_contract,
        bias_contract,
    ) = params
    start_value = source.astype(jnp.float32)
    norm_one, unit_one, inv_one = layer_norm_parts(start_value, gain_one, shift_one)
    normed_first = norm_one.astype(jnp.bfloat16)
    projected = (
        jnp.einsum("td,kdh->kth", normed_first, weight_qkv, preferred_element_type=jnp.float32)
        + bias_qkv[:, None, :]
    )
    query_rot = rotate_pairs(projected[0], cosine, sine_val)
    key_rot = rotate_pairs(projected[1], cosine, sine_val)
    query_low = query_rot.astype(jnp.bfloat16)
    key_low = key_rot.astype(jnp.bfloat16)
    value_low = projected[2].astype(jnp.bfloat16)
    attended, log_sum = attend_forward(query_low, key_low, value_low, segment, cosine.shape[1])
    attended_low = attended.astype(jnp.bfloat16)
    branch = (
        lax.psum(jnp.dot(attended_low, weight_proj, preferred_element_type=jnp.float32), "head")
        + bias_proj
    )
    middle = start_value + branch
    norm_two, unit_two, inv_two = layer_norm_parts(middle, gain_two, shift_two)
    normed_second = norm_two.astype(jnp.bfloat16)
    hidden = jnp.dot(normed_second, weight_expand, preferred_element_type=jnp.float32) + bias_expand
    active_low = jax.nn.gelu(hidden, approximate=False).astype(jnp.bfloat16)
    branch_two = (
        lax.psum(jnp.dot(active_low, weight_contract, preferred_element_type=jnp.float32), "head")
        + bias_contract
    )
    outcome = middle + branch_two
    return (
        unit_one,
        inv_one,
        normed_first,
        query_rot,
        key_rot,
        query_low,
        key_low,
        value_low,
        log_sum,
        attended_low,
        unit_two,
        inv_two,
        normed_second,
        hidden,
        active_low,
        outcome,
    )


def body(
    patches,
    image_grids,
    out_grad,
    first_gain,
    first_shift,
    qkv_weight,
    qkv_bias,
    rope_freqs,
    proj_weight,
    proj_bias,
    second_gain,
    second_shift,
    expand_weight,
    expand_bias,
    contract_weight,
    contract_bias,
):
    row_count = patches.shape[0]
    head_count = rope_freqs.shape[1]
    segment, grid_row, grid_col, real_row = positions(image_grids, row_count)
    turn_angle = (
        grid_row[:, None, None] * rope_freqs[0][None]
        + grid_col[:, None, None] * rope_freqs[1][None]
    )
    cosine = jnp.cos(turn_angle)
    sine_val = jnp.sin(turn_angle)
    params = (
        first_gain,
        first_shift,
        qkv_weight,
        qkv_bias,
        proj_weight,
        proj_bias,
        second_gain,
        second_shift,
        expand_weight,
        expand_bias,
        contract_weight,
        contract_bias,
    )
    saved = run_forward(patches, params, cosine, sine_val, segment)
    mixed_out = saved[15].astype(jnp.bfloat16)
    fresh = lax.optimization_barrier((patches, params, mixed_out))
    saved = run_forward(fresh[0], fresh[1], cosine, sine_val, segment)
    (
        unit_one,
        inv_one,
        normed_first,
        query_rot,
        key_rot,
        query_low,
        key_low,
        value_low,
        log_sum,
        attended_low,
        unit_two,
        inv_two,
        normed_second,
        hidden,
        active_low,
        outcome,
    ) = saved
    cot_low = out_grad * real_row[:, None].astype(jnp.bfloat16)
    cot_value = cot_low.astype(jnp.float32)
    contract_bias_grad = jnp.sum(cot_value, axis=0)
    contract_grad = jnp.einsum("tf,td->fd", active_low, cot_low, preferred_element_type=jnp.float32)
    active_grad = jnp.einsum(
        "td,fd->tf", cot_low, contract_weight, preferred_element_type=jnp.float32
    )
    gelu_value, gelu_pull = jax.vjp(partial(jax.nn.gelu, approximate=False), hidden)
    hidden_grad = gelu_pull(active_grad)[0].astype(jnp.bfloat16)
    expand_bias_grad = jnp.sum(hidden_grad.astype(jnp.float32), axis=0)
    expand_grad = jnp.einsum(
        "td,tf->df", normed_second, hidden_grad, preferred_element_type=jnp.float32
    )
    second_grad = lax.psum(
        jnp.einsum("tf,df->td", hidden_grad, expand_weight, preferred_element_type=jnp.float32),
        "head",
    )
    second_gain_grad = jnp.sum(second_grad * unit_two, axis=0)
    second_shift_grad = jnp.sum(second_grad, axis=0)
    middle_grad = cot_value + norm_back(second_grad, unit_two, inv_two, second_gain)
    middle_low = middle_grad.astype(jnp.bfloat16)
    proj_bias_grad = jnp.sum(middle_low.astype(jnp.float32), axis=0)
    proj_grad = jnp.einsum(
        "th,td->hd", attended_low, middle_low, preferred_element_type=jnp.float32
    )
    attended_grad = jnp.einsum(
        "td,hd->th", middle_low, proj_weight, preferred_element_type=jnp.float32
    ).astype(jnp.bfloat16)
    query_rot_grad, key_rot_grad, value_grad = attend_backward(
        query_low, key_low, value_low, attended_grad, log_sum, segment, head_count
    )
    query_in_grad, query_angle = rotate_back(query_rot_grad, query_rot, cosine, sine_val)
    key_in_grad, key_angle = rotate_back(key_rot_grad, key_rot, cosine, sine_val)
    angle_grad = query_angle + key_angle
    rope_freqs_grad = jnp.stack(
        [
            jnp.einsum("t,thf->hf", grid_row, angle_grad, precision=lax.Precision.HIGHEST),
            jnp.einsum("t,thf->hf", grid_col, angle_grad, precision=lax.Precision.HIGHEST),
        ]
    )
    qkv_grad_low = jnp.stack([query_in_grad, key_in_grad, value_grad]).astype(jnp.bfloat16)
    qkv_bias_grad = jnp.sum(qkv_grad_low.astype(jnp.float32), axis=1)
    qkv_grad = jnp.einsum(
        "td,kth->kdh", normed_first, qkv_grad_low, preferred_element_type=jnp.float32
    )
    first_grad = lax.psum(
        jnp.einsum("kth,kdh->td", qkv_grad_low, qkv_weight, preferred_element_type=jnp.float32),
        "head",
    )
    first_gain_grad = jnp.sum(first_grad * unit_one, axis=0)
    first_shift_grad = jnp.sum(first_grad, axis=0)
    patches_grad = middle_grad + norm_back(first_grad, unit_one, inv_one, first_gain)
    qkv_sum, proj_sum, expand_sum, contract_sum = (
        lax.psum_scatter(qkv_grad, "dp", scatter_dimension=1, tiled=True),
        lax.psum_scatter(proj_grad, "dp", scatter_dimension=1, tiled=True),
        lax.psum_scatter(expand_grad, "dp", scatter_dimension=0, tiled=True),
        lax.psum_scatter(contract_grad, "dp", scatter_dimension=1, tiled=True),
    )
    (
        first_gain_sum,
        first_shift_sum,
        qkv_bias_sum,
        rope_freqs_sum,
        proj_bias_sum,
        second_gain_sum,
        second_shift_sum,
        expand_bias_sum,
        contract_bias_sum,
    ) = lax.psum(
        (
            first_gain_grad,
            first_shift_grad,
            qkv_bias_grad,
            rope_freqs_grad,
            proj_bias_grad,
            second_gain_grad,
            second_shift_grad,
            expand_bias_grad,
            contract_bias_grad,
        ),
        "dp",
    )
    return (
        mixed_out,
        patches_grad,
        qkv_sum,
        proj_sum,
        expand_sum,
        contract_sum,
        first_gain_sum,
        first_shift_sum,
        qkv_bias_sum,
        rope_freqs_sum,
        proj_bias_sum,
        second_gain_sum,
        second_shift_sum,
        expand_bias_sum,
        contract_bias_sum,
    )


def solution(mesh):
    in_specs = (
        P("dp", None),
        P("dp", None),
        P("dp", None),
        P(),
        P(),
        P(None, None, "head"),
        P(None, "head"),
        P(None, "head", None),
        P("head", None),
        P(),
        P(),
        P(),
        P(None, "head"),
        P("head"),
        P("head", None),
        P(),
    )
    out_specs = (
        P("dp", None),
        P("dp", None),
        P(None, "dp", "head"),
        P("head", "dp"),
        P("dp", "head"),
        P("head", "dp"),
        P(),
        P(),
        P(None, "head"),
        P(None, "head", None),
        P(),
        P(),
        P(),
        P("head"),
        P(),
    )
    return jax.shard_map(body, mesh=mesh, in_specs=in_specs, out_specs=out_specs, check_vma=False)
```

profile of v0, /device:TPU:0, one launch (start us, length us, event | category | flops | bytes accessed | tf_op | source)
XLA Modules:
  0.0 1078.4 jit_solution(5829515903000823336)
XLA Ops:
  29.6 64.2 %while.37 = (s32[]{:T(128)}, bf16[2,512,6,64]{1,3,2,0:T(8,128)(2,1)}, s32[2,512]{1,0:T(2,128)S(1)}, s32[1024]{0:T(1024)S(1)}, bf16[2,512,6,64]{1,3,2,0:T(8,128)(...) while((s32[]{:T(128)}, bf16[2,512,6,64]{1,3,2,0:T(8,128)(2,1)}, ...), condition=%wide.region_9.10_spmd, body=%wide.region_6.9_spmd.sunk | while | flops 830997504 | bytes 63609020 | solution.py:111
  30.0 7.4 fusion.243
  37.4 16.7 %fusion.244 = (f32[6,512]{1,0:T(8,128)S(1)}, f32[6,512,1024]{2,1,0:T(8,128)}) fusion(f32[6,512,1024]{2,1,0:T(8,128)} %fusion.243, pred[512,1024]{1,0:T(8,128)(4,1)S(1)} %broadcast_compare_fusion.8), kind=kOutput, calls=%fused_computation.303.clone.1 | output fusion | flops 18875392 | bytes 25702400 | tf_op jit(solution)/shard_map/while/body/eval_jaxpr/sub | solution.py:103
  62.1 7.4 fusion.243
  69.5 16.7 %fusion.244 = (f32[6,512]{1,0:T(8,128)S(1)}, f32[6,512,1024]{2,1,0:T(8,128)}) fusion(f32[6,512,1024]{2,1,0:T(8,128)} %fusion.243, pred[512,1024]{1,0:T(8,128)(4,1)S(1)} %broadcast_compare_fusion.8), kind=kOutput, calls=%fused_computation.303.clone.1 | output fusion | flops 18875392 | bytes 25702400 | tf_op jit(solution)/shard_map/while/body/eval_jaxpr/sub | solution.py:103
  98.7 26.1 %all-reduce.9.cloned.1.call-done = f32[1024,768]{1,0:T(8,128)} async-done(((f32[1024,768]{1,0:T(8,128)}), f32[1024,768]{1,0:T(8,128)}) %all-reduce.9.cloned.1.call-update) | async-done | bytes 3145744 | tf_op jit(solution)/shard_map/psum | solution.py:203
  129.5 21.6 %fusion.87 = f32[1024,768]{1,0:T(8,128)} fusion(bf16[1536,768]{1,0:T(8,128)(2,1)} %param.36, bf16[768,1536]{1,0:T(8,128)(2,1)S(1)} %copy-done, f32[1536]{0:T(1024)S(1)} %copy-done.70, f32[768]{0:T(1024)S(1)} %copy-done.77, f32[768]{0:T(1024)S(1)} %copy-done.56, f32[1024]{0:T(1024)S(1)} %add_rsqrt_fusion.2, f32[1024]{0:T(1024)S(1)} %broadcast_multiply_fusion.6, ...), kind=kOutput, calls=%fused_computation.148 | convolution fusion | flops 4941938688 | bytes 12606464 | tf_op jit(solution)/shard_map/dot_general | solution.py:212
  151.2 24.6 %all-reduce.11.cloned.1.call-done = f32[1024,768]{1,0:T(8,128)} async-done(((f32[1024,768]{1,0:T(8,128)}), f32[1024,768]{1,0:T(8,128)}) %all-reduce.11.cloned.1.call-update) | async-done | bytes 3145744 | tf_op jit(solution)/shard_map/psum | solution.py:212
  198.6 25.5 %while.38 = (s32[]{:T(128)}, bf16[2,512,6,64]{1,3,2,0:T(8,128)(2,1)}, f32[2,6,512]{2,1,0:T(8,128)S(1)}, s32[2,512]{1,0:T(2,128)S(1)}, s32[1024]{0:T(1024)S(1)}, ...) while((s32[]{:T(128)}, ...), condition=%wide.region_19.20_spmd, body=%wide.region_16.19_spmd.sunk | while | flops 843576320 | bytes 52164808 | solution.py:111
  230.1 24.4 %all-reduce.13.cloned.1.call-done = f32[1024,768]{1,0:T(8,128)} async-done(((f32[1024,768]{1,0:T(8,128)}), f32[1024,768]{1,0:T(8,128)}) %all-reduce.13.cloned.1.call-update) | async-done | bytes 3145744 | tf_op jit(solution)/shard_map/psum | solution.py:203
  257.9 15.1 %fusion.51 = (f32[1024,1536]{1,0:T(8,128)S(1)}, f32[1024,1536]{1,0:T(8,128)S(1)}) fusion(f32[1536]{0:T(1024)S(1)} %copy-done.70, bf16[768,1536]{1,0:T(8,128)(2,1)S(1)} %copy-done, f32[1024,768]{1,0:T(8,128)S(1)} %get-tuple-element.484, f32[768]{0:T(1024)S(1)} %copy-done.77, f32[768]{0:T(1024)S(1)} %copy-done.56, f32[1024]{0:T(1024)S(1)} %add_rsqrt_fusion, ...), kind=kOutput, calls=%fused_computation.70 | convolution fusion | flops 2518941696 | bytes 18108416 | tf_op jit(solution)/shard_map/dot_general | solution.py:209
  284.9 24.6 %all-reduce.15.cloned.1.call-done = f32[1024,768]{1,0:T(8,128)} async-done(((f32[1024,768]{1,0:T(8,128)}), f32[1024,768]{1,0:T(8,128)}) %all-reduce.15.cloned.1.call-update) | async-done | bytes 3145744 | tf_op jit(solution)/shard_map/psum | solution.py:312
  329.3 87.9 %while.39 = (s32[]{:T(128)}, f32[1024,6,64]{0,2,1:T(8,128)}, f32[1024,6,64]{0,2,1:T(8,128)}, f32[2,512,6,64]{1,0,3,2:T(2,128)}, bf16[2,512,6,64]{1,3,2,0:T(8,128...) while((s32[]{:T(128)}, f32[1024,6,64]{0,2,1:T(8,128)}, ...), condition=%wide.region_28.29_spmd.clone, body=%wide.region_26.28_spmd.clone.sunk | while | flops 2063135744 | bytes 132749616 | solution.py:162
  337.6 7.1 multiply_reduce_fusion.8
  357.9 15.0 %dynamic_update_slice.25 = f32[2,512,6,64]{1,0,3,2:T(2,128)} dynamic-update-slice(f32[2,512,6,64]{1,0,3,2:T(2,128)} %get-tuple-element.762, f32[1,512,6,64]{1,0,3,2:T(1,128)} %copy.267, s32[]{:T(128)S(6)} %copy.295, s32[]{:T(128)} %constant.51.clone.1..sunk, s32[]{:T(128)} %constant.51.clone.1..sunk, s32[]{:T(128)} %constant.51.clone.1..sunk) | dynamic-update-slice | bytes 1572868 | tf_op jit(solution)/shard_map/while/body/jit(dynamic_update_index_in_dim)/dynamic_update_slice | solution.py:111
  381.9 7.1 multiply_reduce_fusion.8
  402.2 15.0 %dynamic_update_slice.25 = f32[2,512,6,64]{1,0,3,2:T(2,128)} dynamic-update-slice(f32[2,512,6,64]{1,0,3,2:T(2,128)} %get-tuple-element.762, f32[1,512,6,64]{1,0,3,2:T(1,128)} %copy.267, s32[]{:T(128)S(6)} %copy.295, s32[]{:T(128)} %constant.51.clone.1..sunk, s32[]{:T(128)} %constant.51.clone.1..sunk, s32[]{:T(128)} %constant.51.clone.1..sunk) | dynamic-update-slice | bytes 1572868 | tf_op jit(solution)/shard_map/while/body/jit(dynamic_update_index_in_dim)/dynamic_update_slice | solution.py:111
  462.6 11.4 %fusion.84 = f32[1536,768]{0,1:T(8,128)} fusion(f32[1024,1536]{1,0:T(8,128)} %copy-done.80, f32[1024,1536]{1,0:T(8,128)} %copy-done.81, f32[1536]{0:T(1024)S(1)} %copy-done.71, bf16[1024,768]{1,0:T(8,128)(2,1)} %param.24, bf16[1024]{0:T(1024)(128)(2,1)S(1)} %copy-done.64), kind=kOutput, calls=%fused_computation.133 | convolution fusion | flops 2422996992 | bytes 18882560 | tf_op jit(solution)/shard_map/tf,td->fd/dot_general | solution.py:302
  474.7 7.9 fusion.177
  497.5 79.5 %all-reduce.1 = (f32[768]{0:T(1024)}, f32[768]{0:T(1024)}, f32[3,384]{1,0:T(4,128)}, f32[2,6,32]{2,1,0:T(8,128)S(1)}, f32[768]{0:T(1024)}, /*index=5*/f32[768]{0...) all-reduce(f32[768]{0:T(1024)S(1)} %get-tuple-element.410, ...), channel_id=1, replica_groups=mesh['dp'=16,'head'=2] {'dp'}, use_global_device_ids=true, to_apply=%region_37.38 | all-reduce | flops 7680 | bytes 61440 | tf_op jit(solution)/shard_map/psum | solution.py:367
  582.6 72.6 %all-reduce.19.cloned.1.call-done = f32[3,768,384]{2,0,1:T(4,128)} async-done(((f32[3,768,384]{2,0,1:T(4,128)}), f32[3,768,384]{2,0,1:T(4,128)}) %all-reduce.19.cloned.1.call-update) | async-done | bytes 3538960
  656.9 127.7 %reduce-scatter.4.cloned.1.call-done = f32[384,48]{0,1:T(8,128)} async-done(((f32[384,768]{0,1:T(8,128)}), f32[384,48]{0,1:T(8,128)}) %reduce-scatter.4.cloned.1.call-update) | async-done | bytes 73744 | tf_op jit(solution)/shard_map/reduce_scatter | solution.py:353
  784.6 143.5 %reduce-scatter.8.cloned.1.call-done = f32[1536,48]{0,1:T(8,128)} async-done(((f32[1536,768]{0,1:T(8,128)}), f32[1536,48]{0,1:T(8,128)}) %reduce-scatter.8.cloned.1.call-update) | async-done | bytes 294928 | tf_op jit(solution)/shard_map/reduce_scatter | solution.py:355
  928.1 143.6 %reduce-scatter.6.cloned.1.call-done = f32[48,1536]{1,0:T(8,128)} async-done(((f32[768,1536]{1,0:T(8,128)}), f32[48,1536]{1,0:T(8,128)}) %reduce-scatter.6.cloned.1.call-update) | async-done | bytes 294928 | tf_op jit(solution)/shard_map/reduce_scatter | solution.py:354
  (339 shorter events, 246.8 us)
Async XLA Ops:
  7.2 122.3 %copy-start = (bf16[768,1536]{1,0:T(8,128)(2,1)S(1)}, bf16[768,1536]{1,0:T(8,128)(2,1)}, u32[]{:S(2)}) copy-start(bf16[768,1536]{1,0:T(8,128)(2,1)} %param.34) | copy-start | bytes 7077892
  7.2 117.6 %all-reduce.9.cloned.1.call-start = ((), (), s32[]{:S(2)}) async-start(), calls=%async_computation.3 | async-start | bytes 6291456 | tf_op jit(solution)/shard_map/psum | solution.py:203
  37.4 16.7 %copy-start.25 = (bf16[2,512,6,64]{1,3,2,0:T(8,128)(2,1)S(1)}, bf16[2,512,6,64]{1,3,2,0:T(8,128)(2,1)}, u32[]{:S(2)}) copy-start(bf16[2,512,6,64]{1,3,2,0:T(8,128)(2,1)} %get-tuple-element.704) | copy-start | bytes 2359300 | tf_op jit(solution)/shard_map/while
  37.4 16.7 %copy-start.32 = (bf16[1024,6,64]{0,2,1:T(8,128)(2,1)S(1)}, bf16[1024,6,64]{0,2,1:T(8,128)(2,1)}, u32[]{:S(2)}) copy-start(bf16[1024,6,64]{0,2,1:T(8,128)(2,1)} %get-tuple-element.717) | copy-start | bytes 2359300 | tf_op jit(solution)/shard_map/while
  69.5 16.7 %copy-start.25 = (bf16[2,512,6,64]{1,3,2,0:T(8,128)(2,1)S(1)}, bf16[2,512,6,64]{1,3,2,0:T(8,128)(2,1)}, u32[]{:S(2)}) copy-start(bf16[2,512,6,64]{1,3,2,0:T(8,128)(2,1)} %get-tuple-element.704) | copy-start | bytes 2359300 | tf_op jit(solution)/shard_map/while
  69.5 16.7 %copy-start.32 = (bf16[1024,6,64]{0,2,1:T(8,128)(2,1)S(1)}, bf16[1024,6,64]{0,2,1:T(8,128)(2,1)}, u32[]{:S(2)}) copy-start(bf16[1024,6,64]{0,2,1:T(8,128)(2,1)} %get-tuple-element.717) | copy-start | bytes 2359300 | tf_op jit(solution)/shard_map/while
  96.0 28.9 %copy-start.49 = (f32[768]{0:T(1024)S(1)}, f32[768]{0:T(1024)}, u32[]{:S(2)}) copy-start(f32[768]{0:T(1024)} %param.31) | copy-start | bytes 9220
  98.7 77.1 %all-reduce.11.cloned.1.call-start = ((), (), s32[]{:S(2)}) async-start(), calls=%async_computation.4 | async-start | bytes 6291456 | tf_op jit(solution)/shard_map/psum | solution.py:212
  151.1 24.7 %copy-start.67 = (f32[768]{0:T(1024)S(1)}, f32[768]{0:T(1024)}, u32[]{:S(2)}) copy-start(f32[768]{0:T(1024)} %param.37) | copy-start | bytes 9220
  151.1 103.4 %all-reduce.13.cloned.1.call-start = ((), (), s32[]{:S(2)}) async-start(), calls=%async_computation.5 | async-start | bytes 6291456 | tf_op jit(solution)/shard_map/psum | solution.py:203
  229.9 79.5 %all-reduce.15.cloned.1.call-start = ((), (), s32[]{:S(2)}) async-start(), calls=%async_computation.6 | async-start | bytes 6291456 | tf_op jit(solution)/shard_map/psum | solution.py:312
  257.4 15.7 %copy-start.9 = (f32[1024,768]{1,0:T(8,128)}, f32[1024,768]{1,0:T(8,128)S(1)}, u32[]{:S(2)}) copy-start(f32[1024,768]{1,0:T(8,128)S(1)} %get-tuple-element.484) | copy-start | bytes 9437188
  257.4 56.5 %copy-start.47 = (f32[1024]{0:T(1024)}, f32[1024]{0:T(1024)S(1)}, u32[]{:S(2)}) copy-start(f32[1024]{0:T(1024)S(1)} %broadcast_multiply_fusion.4) | copy-start | bytes 12292
  257.9 56.0 %copy-start.52 = (f32[1024]{0:T(1024)}, f32[1024]{0:T(1024)S(1)}, u32[]{:S(2)}) copy-start(f32[1024]{0:T(1024)S(1)} %add_rsqrt_fusion) | copy-start | bytes 12292
  257.9 15.2 %copy-start.31 = (bf16[1024,768]{1,0:T(8,128)(2,1)S(1)}, bf16[1024,768]{1,0:T(8,128)(2,1)}, u32[]{:S(2)}) copy-start(bf16[1024,768]{1,0:T(8,128)(2,1)} %param.24) | copy-start | bytes 4718596
  257.9 15.2 %copy-start.63 = (bf16[1024]{0:T(1024)(128)(2,1)S(1)}, bf16[1024]{0:T(1024)(128)(2,1)}, u32[]{:S(2)}) copy-start(bf16[1024]{0:T(1024)(128)(2,1)} %get-tuple-element.481) | copy-start | bytes 6148
  257.9 15.2 %copy-start.68 = (bf16[1536,768]{1,0:T(8,128)(2,1)S(1)}, bf16[1536,768]{1,0:T(8,128)(2,1)}, u32[]{:S(2)}) copy-start(bf16[1536,768]{1,0:T(8,128)(2,1)} %param.36) | copy-start | bytes 7077892
  284.8 209.4 %all-reduce.17.cloned.1.call-start = ((), (), s32[]{:S(2)}) async-start(), calls=%async_computation.7 | async-start | bytes 6291456 | tf_op jit(solution)/shard_map/psum | solution.py:344
  443.9 211.3 %all-reduce.19.cloned.1.call-start = ((), (), s32[]{:S(2)}) async-start(), calls=%async_computation.11 | async-start | bytes 9437184
  457.2 327.3 %reduce-scatter.4.cloned.1.call-start = ((), (), s32[]{:S(2)}) async-start(), calls=%async_computation.8 | async-start | bytes 1253376 | tf_op jit(solution)/shard_map/reduce_scatter | solution.py:353
  462.3 465.8 %reduce-scatter.8.cloned.1.call-start = ((), (), s32[]{:S(2)}) async-start(), calls=%async_computation.10 | async-start | bytes 5013504 | tf_op jit(solution)/shard_map/reduce_scatter | solution.py:355
  474.0 597.6 %reduce-scatter.6.cloned.1.call-start = ((), (), s32[]{:S(2)}) async-start(), calls=%async_computation.9 | async-start | bytes 5013504 | tf_op jit(solution)/shard_map/reduce_scatter | solution.py:354
  484.5 9.2 copy-start.28
  484.5 9.2 copy-start.29
  (79 other events, 233.5 us)
Sparse Core Ops, SparseCore 0:
  98.8 26.0 all-reduce.8
  151.2 24.5 all-reduce.10
  230.0 24.4 all-reduce.12
  284.9 24.4 all-reduce.14
  444.0 24.4 all-reduce.16
  474.1 181.0 all-reduce.18
  660.5 124.0 reduce-scatter.3
  790.3 137.6 reduce-scatter.7
  933.8 137.7 reduce-scatter.5
where the time goes:
time: 1090 us; the launch traced here: 1080 us
  waiting for transfers between devices  587 us (54%)
  matrix products  180 us (17%)
  other arithmetic  121 us (11%)
  local copies, waits for them, and re-layouts  93.3 us (9%)
  blocking collectives  79.5 us (7%)
  between operations  15.7 us (1%)
    reduce_scatter x1, waiting for transfers between devices, body(): lax.psum_scatter(expand_grad, 'dp', scatter_dimension=0, tiled=True)  144 us
    reduce_scatter x1, waiting for transfers between devices, body(): lax.psum_scatter(contract_grad, 'dp', scatter_dimension=1, tiled=True)  143 us
    reduce_scatter x1, waiting for transfers between devices, body(): lax.psum_scatter(proj_grad, 'dp', scatter_dimension=1, tiled=True)  128 us
    psum x1, blocking collectives, body(): lax.psum((first_gain_grad, first_shift_grad, qkv_bias_grad, rope_freqs_gr...  79.5 us
    unnamed x10, waiting for transfers between devices  72.7 us
    psum x2, waiting for transfers between devices, run_forward(): lax.psum(jnp.dot(attended_low, weight_proj, preferred_element_type=jnp.fl...  50.6 us
    sub x2, other arithmetic, one_block(): exp_scores = jnp.exp(scores - row_max)  33.5 us
    dynamic_update_slice x4, local copies, waits for them, and re-layouts, attend_forward(): block_outs, log_sum = lax.map(one_block, (query_blocks, segment_blocks))  33.3 us
  transfers between devices with their start and end apart: 9, of which 8 were waited for; matrix products, arithmetic and copies ran while one was open for 5% of the time, Pallas kernels for 0%

commit v1 on v0

v1 whole, which is shorter than its diff:
```python
from functools import partial

import jax
import jax.numpy as jnp
from jax import lax
from jax.experimental import pallas as pl
from jax.experimental.pallas import tpu as pltpu
from jax.sharding import PartitionSpec as P

F32 = jnp.float32
BF16 = jnp.bfloat16
EPS = 1e-06
FAR = 2.0**100
R = 256
SUB = 64
PAIR = 128
HALF = 64
CHUNK = 256
MESH = pl.DeviceIdType.MESH
ANY = pl.ANY


def dot_nn(a, b):
    return lax.dot_general(a, b, (((1,), (0,)), ((), ())), preferred_element_type=F32)


def dot_nt(a, b):
    return lax.dot_general(a, b, (((1,), (1,)), ((), ())), preferred_element_type=F32)


def aligned(i, size):
    return pl.ds(pl.multiple_of(i * size, size), size)


def loop(count, fn):
    def step(i, carry):
        fn(i)
        return carry

    lax.fori_loop(0, count, step, 0)


def unit_of(rows):
    centred = rows - jnp.mean(rows, axis=-1, keepdims=True)
    inv = lax.rsqrt(jnp.mean(centred * centred, axis=-1, keepdims=True) + EPS)
    return centred * inv, inv


def norm_back(upstream, unit, inv, gain):
    scaled = upstream * gain
    return inv * (
        scaled
        - jnp.mean(scaled, axis=-1, keepdims=True)
        - unit * jnp.mean(scaled * unit, axis=-1, keepdims=True)
    )


def swap_halves(v, lane_first):
    return jnp.where(lane_first, pltpu.roll(v, PAIR - HALF // 2, 1), pltpu.roll(v, HALF // 2, 1))


def lane_ids(rows):
    return lax.broadcasted_iota(jnp.int32, (rows, PAIR), 1)


def head_mask(h):
    lane = lax.broadcasted_iota(jnp.int32, (1, PAIR), 1)
    return (lane // HALF == h).astype(F32)


def front_kernel(
    grids, x, gain, shift, w, b, freqs,
    q8, key, val, nf, att, lse, ohq, ohk, cos, sin, pos,
    kx, lcol,
):
    rows_all = x.shape[0]
    slots = grids.shape[0]
    pairs = q8.shape[1] // PAIR
    side = lax.broadcasted_iota(jnp.int32, (32, 1), 0).astype(F32)
    ang_r = side * freqs[0:1, :]
    ang_c = side * freqs[1:2, :]
    table_r = jnp.concatenate([jnp.cos(ang_r), jnp.sin(ang_r)], axis=1)
    table_c = jnp.concatenate([jnp.cos(ang_c), jnp.sin(ang_c)], axis=1)
    width_all = q8.shape[1]

    def first(r):
        rows = aligned(r, R)
        t = lax.broadcasted_iota(jnp.int32, (R, 1), 0) + r * R
        seg = jnp.zeros((R, 1), jnp.int32)
        start = jnp.zeros((R, 1), jnp.int32)
        width = jnp.ones((R, 1), jnp.int32)
        end = jnp.int32(0)
        for s in range(slots):
            begin = end
            end = end + grids[s, 0] * grids[s, 1]
            inside = (t >= begin) & (t < end)
            start = jnp.where(inside, begin, start)
            width = jnp.where(inside, grids[s, 1], width)
            seg = seg + (t >= end).astype(jnp.int32)
        real = (seg < slots).astype(F32)
        off = (t - start).astype(F32)
        wide = width.astype(F32)
        grow = jnp.floor((off + 0.5) / wide) * real
        gcol = (off - grow * wide) * real
        lane = lane_ids(R)
        pos[rows, :] = (
            jnp.where(lane == 0, real, 0.0)
            + jnp.where(lane == 1, grow, 0.0)
            + jnp.where(lane == 2, gcol, 0.0)
        )
        hot = (lane % HALF == seg).astype(F32)
        ohq[rows, :] = hot.astype(BF16)
        ohk[rows, :] = ((1.0 - hot) * (-FAR)).astype(BF16)
        spot = lax.broadcasted_iota(jnp.int32, (R, 32), 1)
        hot_r = (spot == grow.astype(jnp.int32)).astype(F32)
        hot_c = (spot == gcol.astype(jnp.int32)).astype(F32)
        got_r = jnp.dot(hot_r, table_r, precision=lax.Precision.HIGHEST, preferred_element_type=F32)
        got_c = jnp.dot(hot_c, table_c, precision=lax.Precision.HIGHEST, preferred_element_type=F32)
        cr, sr = got_r[:, :width_all], got_r[:, width_all:]
        cc, sc = got_c[:, :width_all], got_c[:, width_all:]
        cos[rows, :] = cr * cc - sr * sc
        sin[rows, :] = sr * cc + cr * sc
        unit, _ = unit_of(x[rows, :].astype(F32))
        normed = (unit * gain[...] + shift[...]).astype(BF16)
        nf[rows, :] = normed
        lane_first = lane % HALF < HALF // 2
        sign = jnp.where(lane_first, -1.0, 1.0)
        for k, out in ((0, q8), (1, key)):
            got = dot_nn(normed, w[k]) + b[k : k + 1, :]
            for p in range(pairs):
                cols = slice(p * PAIR, (p + 1) * PAIR)
                part = got[:, cols]
                turned = part * cos[rows, cols] + swap_halves(part, lane_first) * (
                    sin[rows, cols] * sign
                )
                turned = turned.astype(BF16)
                if k == 0:
                    turned = turned * jnp.asarray(HALF**-0.5, BF16)
                out[rows, cols] = turned
        val[rows, :] = (dot_nn(normed, w[2]) + b[2:3, :]).astype(BF16)

    loop(rows_all // R, first)

    def heads(p):
        cols = aligned(p, PAIR)
        for h in range(2):
            mine = head_mask(h).astype(BF16)
            other = head_mask(1 - h).astype(BF16)
            kx[...] = key[:, cols] * mine + ohk[...] * other

            def queries(r, h=h, mine=mine, other=other):
                rows = aligned(r, R)
                qx = q8[rows, cols] * mine + ohq[rows, :] * other
                score = dot_nt(qx, kx[...])
                top = jnp.max(score, axis=-1, keepdims=True)
                grown = jnp.exp(score - top)
                total = jnp.sum(grown, axis=-1, keepdims=True)
                got = dot_nn(grown.astype(BF16), val[:, cols]) * (1.0 / total)
                lane = lane_ids(R)
                log_sum = top + jnp.log(total)
                if h == 0:
                    att[rows, cols] = got
                else:
                    att[rows, cols] = jnp.where(lane < HALF, att[rows, cols], got)
                lcol[rows, :] = jnp.where(lane == p * 2 + h, log_sum, lcol[rows, :])

            loop(rows_all // R, queries)

    loop(pairs, heads)

    def turn(r):
        rows = aligned(r, PAIR)
        lse[:, rows] = jnp.transpose(lcol[rows, :])[: lse.shape[0], :]

    loop(rows_all // PAIR, turn)


def front(grids, x, gain, shift, w, b, freqs):
    rows, width = x.shape
    cols = w.shape[2]
    shape = jax.ShapeDtypeStruct
    vm = pl.BlockSpec(memory_space=pltpu.VMEM)
    outs = [
        shape((rows, cols), BF16), shape((rows, cols), BF16), shape((rows, cols), BF16),
        shape((rows, width), BF16), shape((rows, cols), F32), shape((8, rows), F32),
        shape((rows, PAIR), BF16), shape((rows, PAIR), BF16),
        shape((rows, cols), F32), shape((rows, cols), F32), shape((rows, PAIR), F32),
    ]
    return pl.pallas_call(
        front_kernel,
        name="front",
        out_shape=outs,
        in_specs=[pl.BlockSpec(memory_space=pltpu.SMEM)] + [vm] * 6,
        out_specs=[vm] * len(outs),
        scratch_shapes=[pltpu.VMEM((rows, PAIR), BF16), pltpu.VMEM((rows, PAIR), F32)],
        compiler_params=pltpu.CompilerParams(vmem_limit_bytes=48 << 20),
    )(grids, x, gain, shift, w, b, freqs)


PARTS = 16


def main_kernel(
    fuse, pairs, chunks,
    att_h, q8_h, key_h, val_h, nf_h, ohq_h, ohk_h, cos_h, sin_h, lse_h, pos_h,
    x_h, og_h, wp_h, we_h, wc_h, wq_h,
    bias_p, gain_two, shift_two, bias_e, bias_c, gain_one,
    mixed_h, pgrad_h, ff_h, pq_h, small_h,
    att, q8, key, val, ohq, ohk, lse, pos, x, cot, wp, we, wc,
    acc_a, acc_b, xbuf, mid, cott, ns, nst, act, hgb, dgrad, delta,
    km, vm, kt, kmt, dk, dv, dqt, qkvg, cos, sin, sums,
    gf, gq, r1, r2, r3, small, small_r,
    lsem, xs, xr, credit, s1, e1, s2, e2, s3, e3, c1, c2, c3, ms, mr, osem,
):
    me = lax.axis_index("dp")
    core = lax.axis_index("head")
    blocks = x.shape[0] // R
    subs = x.shape[0] // SUB
    mate = (me, 1 - core)
    if fuse:
        xx, yy, zz = me % 2, (me // 2) % 2, me // 4
        fst = xx * (1 - core) + yy * core
        snd = yy * (1 - core) + xx * core
        peer1 = (me + (1 - 2 * fst) * (1 + core), core)
        peer2 = (me + (1 - 2 * snd) * (2 - core), core)
        peers_z = [(((zz + j) % 4) * 4 + me % 4, core) for j in (1, 2, 3)]

        def where(z, f, s):
            return z * 4 + s * (2 - core) + f * (1 + core)

    def load(src, dst, i):
        copy = pltpu.make_async_copy(src, dst, lsem.at[i])
        copy.start()
        return copy

    get_att = load(att_h, att, 0)
    get_wp = load(wp_h, wp, 1)
    get_og = load(og_h, cot, 2)
    get_pos = load(pos_h, pos, 3)
    get_x = load(x_h, x, 4)
    get_we = load(we_h, we, 5)
    get_wc = load(wc_h, wc, 6)
    get_late = [
        load(q8_h, q8, 7), load(key_h, key, 8), load(val_h, val, 9),
        load(ohq_h, ohq, 10), load(ohk_h, ohk, 11), load(lse_h, lse, 12),
    ]

    barrier = pltpu.get_barrier_semaphore()
    friends = [mate] + ([peer1, peer2] + peers_z if fuse else [])
    for friend in friends:
        pl.semaphore_signal(barrier, inc=1, device_id=friend, device_id_type=MESH)
    pl.semaphore_wait(barrier, len(friends))

    def exchange(src, r):
        return pltpu.make_async_remote_copy(
            src.at[aligned(r, R), :], xbuf.at[aligned(r, R), :], xs.at[r], xr.at[r],
            device_id=mate, device_id_type=MESH,
        )

    def send(src, r):
        exchange(src, r).start()

    def give_credit(r):
        pl.semaphore_signal(credit.at[r], inc=1, device_id=mate, device_id_type=MESH)

    def take_credit(r):
        pl.semaphore_wait(credit.at[r], 1)

    def remote(src, dst, ss, rs, peer):
        return pltpu.make_async_remote_copy(
            src, dst, ss, rs, device_id=peer, device_id_type=MESH
        )

    class Line:
        def __init__(self, grads, base, width, out, guard):
            self.g, self.base, self.n, self.out, self.guard = grads, base, width, out, guard

        def buf(self, buf, j, b):
            return buf.at[j, b, :, pl.ds(0, self.n)]

        def whole(self, buf, j):
            return buf.at[j, :, :, pl.ds(0, self.n)]

        def start1(self, j):
            if self.guard == "take":
                pl.semaphore_wait(c1.at[j], 1)

            def one(i):
                remote(
                    self.g.at[j, where(i // 2, 1 - fst, i % 2)], self.buf(r1, j, i),
                    s1.at[self.base + j], e1.at[self.base + j], peer1,
                ).start()

            loop(8, one)

        def give(self, sem, j, peers):
            if self.guard == "give":
                def go():
                    for peer in peers:
                        pl.semaphore_signal(sem.at[j], inc=1, device_id=peer, device_id_type=MESH)
                if isinstance(j, int):
                    if j < 4:
                        go()
                else:
                    pl.when(j < 4)(go)

        def finish1(self, j):
            remote(
                self.g.at[j, pl.ds(0, 8)], self.whole(r1, j),
                s1.at[self.base + j], e1.at[self.base + j], peer1,
            ).wait_recv()

            def one(i):
                b = where(i // 2, fst, i % 2)
                self.g[j, b] = self.g[j, b] + self.buf(r1, j, i)[...]

            loop(8, one)
            self.give(c1, j, [peer1])
            if self.guard == "take":
                pl.semaphore_wait(c2.at[j], 1)

            def two(i):
                remote(
                    self.g.at[j, where(i, fst, 1 - snd)], self.buf(r2, j, i),
                    s2.at[self.base + j], e2.at[self.base + j], peer2,
                ).start()

            loop(4, two)

        def finish2(self, j):
            remote(
                self.g.at[j, pl.ds(0, 4)], self.whole(r2, j),
                s2.at[self.base + j], e2.at[self.base + j], peer2,
            ).wait_recv()

            def one(i):
                b = where(i, fst, snd)
                self.g[j, b] = self.g[j, b] + self.buf(r2, j, i)[...]

            loop(4, one)
            self.give(c2, j, [peer2])
            if self.guard == "take":
                pl.semaphore_wait(c3.at[j], 3)
            for k in range(3):
                remote(
                    self.g.at[j, where((zz + k + 1) % 4, fst, snd)], self.buf(r3, j, k),
                    s3.at[self.base + j], e3.at[self.base + j], peers_z[k],
                ).start()

        def finish3(self, j):
            remote(
                self.g.at[j, pl.ds(0, 3)], self.whole(r3, j),
                s3.at[self.base + j], e3.at[self.base + j], peers_z[0],
            ).wait_recv()
            self.g[j, me] = (
                self.g[j, me]
                + self.buf(r3, j, 0)[...] + self.buf(r3, j, 1)[...] + self.buf(r3, j, 2)[...]
            )
            self.give(c3, j, peers_z)
            pltpu.make_async_copy(self.g.at[j, me], self.out.at[j], osem.at[self.base + j]).start()

        def drain(self, j):
            for src, dst, ss, rs, peer in (
                (self.g.at[j, pl.ds(0, 8)], self.whole(r1, j), s1, e1, peer1),
                (self.g.at[j, pl.ds(0, 4)], self.whole(r2, j), s2, e2, peer2),
                (self.g.at[j, pl.ds(0, 3)], self.whole(r3, j), s3, e3, peers_z[0]),
            ):
                remote(src, dst, ss.at[self.base + j], rs.at[self.base + j], peer).wait_send()
            pltpu.make_async_copy(self.g.at[j, me], self.out.at[j], osem.at[self.base + j]).wait()

    class Plain:
        def __init__(self, grads, base, width, out, guard):
            self.g, self.base, self.out = grads, base, out

        def copy(self, j):
            return pltpu.make_async_copy(self.g.at[j], self.out.at[j], osem.at[self.base + j])

        def start1(self, j):
            self.copy(j).start()

        def finish1(self, j):
            pass

        finish2 = finish3 = finish1

        def drain(self, j):
            self.copy(j).wait()

    kind = Line if fuse else Plain
    ff = kind(gf, 0, 2 * CHUNK, ff_h, "give")
    pq = kind(gq, chunks, 3 * PAIR, pq_h, "take")

    small[...] = jnp.zeros_like(small)
    sums[...] = jnp.zeros_like(sums)

    get_att.wait()
    get_wp.wait()

    def project(r):
        acc_a[aligned(r, R), :] = dot_nn(att[aligned(r, R), :].astype(BF16), wp[...])
        send(acc_a, r)

    loop(blocks, project)

    get_og.wait()
    get_pos.wait()

    def mask_cot(r):
        rows = aligned(r, R)
        block = (cot[rows, :].astype(F32) * pos[rows, 0:1])
        small[0, 0:1, :] = small[0, 0:1, :] + jnp.sum(block, axis=0, keepdims=True)
        low = block.astype(BF16)
        cot[rows, :] = low
        cott[:, rows] = jnp.transpose(low)

    loop(blocks, mask_cot)
    get_x.wait()

    def second_norm(r):
        exchange(acc_a, r).wait()

        def sub(i):
            rows = pl.ds(pl.multiple_of(r * R + i * SUB, SUB), SUB)
            middle = x[rows, :].astype(F32) + ((acc_a[rows, :] + xbuf[rows, :]) + bias_p[...])
            unit, _ = unit_of(middle)
            mid[rows, :] = middle
            ns[rows, :] = (unit * gain_two[...] + shift_two[...]).astype(BF16)
            acc_b[rows, :] = 0.5 * (middle + bias_c[...])
            acc_a[rows, :] = jnp.zeros_like(middle)

        loop(R // SUB, sub)
        give_credit(r)
        nst[:, aligned(r, R)] = jnp.transpose(ns[aligned(r, R), :])

    loop(blocks, second_norm)
    get_we.wait()
    get_wc.wait()

    def feed(j):
        cols = aligned(j, CHUNK)

        def rows_of(r):
            rows = aligned(r, R)
            hidden = dot_nn(ns[rows, :], we[:, cols]) + bias_e[:, cols]
            upstream = dot_nt(cot[rows, :], wc[cols, :])
            phi = 0.5 * (1.0 + lax.erf(hidden * (0.5**0.5)))
            slope = phi + hidden * (jnp.exp(-0.5 * hidden * hidden) * (0.3989422804014327))
            active = (hidden * phi).astype(BF16)
            hgrad = (upstream * slope).astype(BF16)
            act[rows, :] = active
            hgb[rows, :] = hgrad
            sums[0:1, cols] = sums[0:1, cols] + jnp.sum(hgrad.astype(F32), axis=0, keepdims=True)
            acc_b[rows, :] = acc_b[rows, :] + dot_nn(active, wc[cols, :])
            acc_a[rows, :] = acc_a[rows, :] + dot_nt(hgrad, we[:, cols])

        loop(blocks, rows_of)
        got = dot_nn(cott[...], act[...])
        gf[j, :, :, pl.ds(0, CHUNK)] = got.reshape(gf.shape[1], gf.shape[2], CHUNK)
        got = dot_nn(nst[...], hgb[...])
        gf[j, :, :, pl.ds(CHUNK, CHUNK)] = got.reshape(gf.shape[1], gf.shape[2], CHUNK)
        ff.start1(j)

    loop(chunks, feed)

    def send_second(r):
        take_credit(r)
        send(acc_a, r)

    loop(blocks, send_second)
    get_nf = load(nf_h, ns, 0)
    ff.finish1(0)
    ff.finish1(1)

    def second_back(r):
        exchange(acc_a, r).wait()

        def sub(i):
            rows = pl.ds(pl.multiple_of(r * R + i * SUB, SUB), SUB)
            up = acc_a[rows, :] + xbuf[rows, :]
            unit, inv = unit_of(mid[rows, :])
            small[0, 1:2, :] = small[0, 1:2, :] + jnp.sum(up * unit, axis=0, keepdims=True)
            small[0, 2:3, :] = small[0, 2:3, :] + jnp.sum(up, axis=0, keepdims=True)
            grad = cot[rows, :].astype(F32) + norm_back(up, unit, inv, gain_two[...])
            mid[rows, :] = grad
            low = grad.astype(BF16)
            cot[rows, :] = low
            small[0, 3:4, :] = small[0, 3:4, :] + jnp.sum(
                low.astype(F32), axis=0, keepdims=True
            )
            acc_a[rows, :] = jnp.zeros_like(up)

        loop(R // SUB, sub)
        give_credit(r)
        rows = aligned(r, R)
        cott[:, rows] = jnp.transpose(cot[rows, :])
        low = dot_nt(cot[rows, :], wp[...]).astype(BF16)
        dgrad[rows, :] = low
        prod = low.astype(F32) * att[rows, :]
        head = lax.broadcasted_iota(jnp.int32, (8, prod.shape[1]), 0)
        lane = lax.broadcasted_iota(jnp.int32, (8, prod.shape[1]), 1)
        pick = (lane // HALF == head).astype(F32)
        delta[:, rows] = lax.dot_general(
            pick, prod, (((1,), (1,)), ((), ())), precision=lax.Precision.HIGHEST,
            preferred_element_type=F32,
        )

    loop(blocks, second_back)
    gq[0] = dot_nn(cott[...], att[...].astype(BF16)).reshape(gq.shape[1:])
    pq.start1(0)

    def send_mixed(r):
        take_credit(r)
        send(acc_b, r)

    loop(blocks, send_mixed)

    get_nf.wait()

    def turn_first(r):
        nst[:, aligned(r, R)] = jnp.transpose(ns[aligned(r, R), :])

    loop(blocks, turn_first)
    get_wq = [
        load(wq_h.at[k], we.at[:, pl.ds(k * pairs * PAIR, pairs * PAIR)], 4 + k) for k in range(3)
    ]
    for copy in get_late:
        copy.wait()
    kt[...] = jnp.transpose(key[...])

    def mixed_block(r):
        exchange(acc_b, r).wait()
        rows = aligned(r, R)
        ns[rows, :] = (acc_b[rows, :] + xbuf[rows, :]).astype(BF16)
        give_credit(r)
        pltpu.make_async_copy(ns.at[rows, :], mixed_h.at[rows, :], ms.at[r]).start()

    loop(blocks, mixed_block)
    for copy in get_wq:
        copy.wait()

    def pair_back(p):
        cols = aligned(p, PAIR)
        get_cos = load(cos_h.at[:, cols], cos, 0)
        get_sin = load(sin_h.at[:, cols], sin, 1)
        dk[...] = jnp.zeros_like(dk)
        dv[...] = jnp.zeros_like(dv)
        dqt[...] = jnp.zeros_like(dqt)

        def head_back(h):
            mine = head_mask(h).astype(BF16)
            other = head_mask(1 - h).astype(BF16)
            km[...] = key[:, cols] * mine + ohk[...] * other
            vm[...] = val[:, cols] * mine
            spot = lax.broadcasted_iota(jnp.int32, (PAIR, 1), 0)
            kmt[...] = kt[cols, :] * (spot // HALF == h).astype(F32).astype(BF16)
            n = p * 2 + h

            def query_back(r):
                rows = aligned(r, R)
                qm = q8[rows, cols] * mine
                qx = qm + ohq[rows, :] * other
                do = dgrad[rows, cols]
                score = dot_nt(km[...], qx)
                prob = jnp.exp(score - lse[pl.ds(n, 1), rows])
                pgrad = dot_nt(vm[...], do)
                sgrad = (prob * (pgrad - delta[pl.ds(n, 1), rows])).astype(BF16)
                dv[...] = dv[...] + dot_nn(prob.astype(BF16), do * mine)
                dk[...] = dk[...] + dot_nn(sgrad, qm)
                dqt[:, rows] = dqt[:, rows] + dot_nn(kmt[...], sgrad)

            loop(blocks, query_back)
            if fuse:
                pl.when(n < 4)(lambda: ff.finish1(n + 2))
                ff.finish2(n)

        loop(2, head_back)
        get_cos.wait()
        get_sin.wait()

        def turn_back(r):
            rows = aligned(r, R)
            lane_first = lane_ids(R) % HALF < HALF // 2
            sign = jnp.where(lane_first, 1.0, -1.0)
            c, s = cos[rows, :], sin[rows, :]
            total = jnp.zeros((R, PAIR), F32)
            grads = []
            scale = HALF**-0.5
            for k, (grad, turned) in enumerate(
                (
                    (jnp.transpose(dqt[:, rows]) * scale, q8[rows, cols].astype(F32) * (1.0 / scale)),
                    (dk[rows, :], key[rows, cols].astype(F32)),
                )
            ):
                swapped = swap_halves(grad, lane_first) * sign
                total = total + swapped * turned
                grads.append((grad * c + swapped * s).astype(BF16))
            grads.append(dv[rows, :].astype(BF16))
            for k, low in enumerate(grads):
                qkvg[rows, k * PAIR : (k + 1) * PAIR] = low
                sums[k + 1 : k + 2, cols] = sums[k + 1 : k + 2, cols] + jnp.sum(
                    low.astype(F32), axis=0, keepdims=True
                )
            for k in range(2):
                sums[k + 4 : k + 5, cols] = sums[k + 4 : k + 5, cols] + jnp.sum(
                    total * pos[rows, k + 1 : k + 2], axis=0, keepdims=True
                )
            weight = jnp.concatenate(
                [we[:, aligned(k * pairs + p, PAIR)] for k in range(3)], axis=1
            )
            acc_a[rows, :] = acc_a[rows, :] + dot_nt(qkvg[rows, :], weight)

        loop(blocks, turn_back)
        gq[p + 1] = dot_nn(nst[...], qkvg[...]).reshape(gq.shape[1:])
        pq.start1(p + 1)
        if fuse:
            pl.when(p == 0)(lambda: pq.finish1(0))
            pl.when(p == 1)(lambda: pq.finish1(1))
            ff.finish3(p * 2)
            ff.finish3(p * 2 + 1)

    loop(pairs, pair_back)

    def first_send(r):
        def sub(i):
            rows = pl.ds(pl.multiple_of(r * R + i * SUB, SUB), SUB)
            unit, _ = unit_of(x[rows, :].astype(F32))
            up = acc_a[rows, :]
            small[0, 6:7, :] = small[0, 6:7, :] + jnp.sum(up * unit, axis=0, keepdims=True)
            small[0, 7:8, :] = small[0, 7:8, :] + jnp.sum(up, axis=0, keepdims=True)

        take_credit(r)
        send(acc_a, r)
        loop(R // SUB, sub)

    loop(blocks, first_send)

    n = chunks * CHUNK // 2
    small[0, 4:5, :] = sums[0:1, 0:n]
    small[0, 5:6, :] = sums[0:1, n : 2 * n]
    m = pairs * PAIR
    for k in range(5):
        small[0, 8 + k : 9 + k, 0:m] = sums[1 + k : 2 + k, 0:m]

    def small_copy(i, k, peer):
        return remote(small.at[k], small_r.at[i], ms.at[4 + i], mr.at[i], peer)

    copy = small_copy(0, 0, mate)
    copy.start()
    if fuse:
        pq.finish2(0)
    copy.wait()
    line = lax.broadcasted_iota(jnp.int32, small.shape[1:], 0)
    small[1] = small[0] + jnp.where((line == 6) | (line == 7), small_r[0], 0.0)
    if fuse:
        copy = small_copy(1, 1, peer1)
        copy.start()
        pq.finish1(2)
        copy.wait()
        small[2] = small[1] + small_r[1]
        copy = small_copy(2, 2, peer2)
        copy.start()
        pq.finish2(1)
        copy.wait()
        small[3] = small[2] + small_r[2]
        copies = [small_copy(3 + k, 3, peers_z[k]) for k in range(3)]
        for copy in copies:
            copy.start()
    last = 4 if fuse else 1

    def first_back(r):
        exchange(acc_a, r).wait()

        def sub(i):
            rows = pl.ds(pl.multiple_of(r * R + i * SUB, SUB), SUB)
            unit, inv = unit_of(x[rows, :].astype(F32))
            up = acc_a[rows, :] + xbuf[rows, :]
            mid[rows, :] = mid[rows, :] + norm_back(up, unit, inv, gain_one[...])

        loop(R // SUB, sub)
        rows = aligned(r, R)
        pltpu.make_async_copy(mid.at[rows, :], pgrad_h.at[rows, :], xs.at[r]).start()

    loop(blocks, first_back)
    if fuse:
        for copy in copies:
            copy.wait()
        small[4] = small[3] + (small_r[3] + small_r[4] + small_r[5])
    out_small = pltpu.make_async_copy(small.at[last], small_h, lsem.at[0])
    out_small.start()
    if fuse:
        pq.finish3(0)
        pq.finish1(3)
        pq.finish2(2)
        pq.finish3(1)
        pq.finish2(3)
        pq.finish3(2)
        pq.finish3(3)
    loop(chunks, ff.drain)
    loop(pairs + 1, pq.drain)
    out_small.wait()

    def finish_out(r):
        rows = aligned(r, R)
        pltpu.make_async_copy(ns.at[rows, :], mixed_h.at[rows, :], ms.at[r]).wait()
        pltpu.make_async_copy(mid.at[rows, :], pgrad_h.at[rows, :], xs.at[r]).wait()

    loop(blocks, finish_out)


def main_call(fuse, parts, big, small_in):
    (att, q8, key, val, nf, ohq, ohk, cos, sin, lse, pos, x, og, wp, we, wc, wq) = big
    rows, width = x.shape
    heads = q8.shape[1]
    hidden = we.shape[1]
    pairs, chunks = heads // PAIR, hidden // CHUNK
    shape = jax.ShapeDtypeStruct
    part_rows = width // parts
    sent = parts if fuse else 0
    if fuse:
        ff_shape, pq_shape = (chunks, part_rows, 2 * CHUNK), (pairs + 1, part_rows, 3 * PAIR)
        grain = (parts, part_rows)
        slots = chunks
    else:
        ff_shape, pq_shape = (chunks, 1, width, 2 * CHUNK), (pairs + 1, 1, width, 3 * PAIR)
        grain = (1, width)
        slots = 1
    outs = [
        shape((rows, width), BF16), shape((rows, width), F32), shape(ff_shape, F32),
        shape(pq_shape, F32), shape((16, width), F32),
    ]
    any_spec = pl.BlockSpec(memory_space=ANY)
    vm_spec = pl.BlockSpec(memory_space=pltpu.VMEM)
    V = pltpu.VMEM
    DMA = pltpu.SemaphoreType.DMA
    REG = pltpu.SemaphoreType.REGULAR
    blocks = rows // R
    lines = chunks + pairs + 1
    recv = (lambda n: V((slots, n, part_rows, 2 * CHUNK), F32)) if fuse else (lambda n: V((1, 1, 8, PAIR), F32))
    scratch = [
        V((rows, heads), F32), V((rows, heads), BF16), V((rows, heads), BF16), V((rows, heads), BF16),
        V((rows, PAIR), BF16), V((rows, PAIR), BF16), V((8, rows), F32), V((rows, PAIR), F32),
        V((rows, width), BF16), V((rows, width), BF16), V((heads, width), BF16),
        V((width, hidden), BF16), V((hidden, width), BF16),
        V((rows, width), F32), V((rows, width), F32), V((rows, width), F32), V((rows, width), F32),
        V((width, rows), BF16), V((rows, width), BF16), V((width, rows), BF16),
        V((rows, CHUNK), BF16), V((rows, CHUNK), BF16), V((rows, heads), BF16), V((8, rows), F32),
        V((rows, PAIR), BF16), V((rows, PAIR), BF16), V((heads, rows), BF16), V((PAIR, rows), BF16),
        V((rows, PAIR), F32), V((rows, PAIR), F32), V((PAIR, rows), F32), V((rows, 3 * PAIR), BF16),
        V((rows, PAIR), F32), V((rows, PAIR), F32), V((8, hidden), F32),
        V((chunks, *grain, 2 * CHUNK), F32), V((pairs + 1, *grain, 3 * PAIR), F32),
        recv(8), recv(4), recv(3), V((5, 16, width), F32), V((6, 16, width), F32),
        DMA((16,)), DMA((blocks,)), DMA((blocks,)), REG((blocks,)),
        DMA((lines,)), DMA((lines,)), DMA((lines,)), DMA((lines,)), DMA((lines,)), DMA((lines,)),
        REG((4,)), REG((4,)), REG((4,)), DMA((10,)), DMA((6,)), DMA((lines,)),
    ]
    return pl.pallas_call(
        partial(main_kernel, fuse, pairs, chunks),
        name="main",
        out_shape=outs,
        in_specs=[any_spec] * len(big) + [vm_spec] * len(small_in),
        out_specs=[any_spec] * len(outs),
        scratch_shapes=scratch,
        compiler_params=pltpu.CompilerParams(
            collective_id=0, has_side_effects=True, vmem_limit_bytes=67043328
        ),
    )(*big, *small_in)


def body(
    fuse, parts,
    patches, image_grids, out_grad, first_gain, first_shift, qkv_weight, qkv_bias, rope_freqs,
    proj_weight, proj_bias, second_gain, second_shift, expand_weight, expand_bias,
    contract_weight, contract_bias,
):
    width = patches.shape[1]
    heads = qkv_weight.shape[2]
    freqs = jnp.concatenate([rope_freqs, rope_freqs], axis=2).reshape(2, heads)
    row = lambda v: v.reshape(1, -1)
    q8, key, val, nf, att, lse, ohq, ohk, cos, sin, pos = front(
        image_grids, patches, row(first_gain), row(first_shift), qkv_weight, qkv_bias, freqs
    )
    mixed, pgrad, ff, pq, small = main_call(
        fuse,
        parts,
        (att, q8, key, val, nf, ohq, ohk, cos, sin, lse, pos, patches, out_grad,
         proj_weight, expand_weight, contract_weight, qkv_weight),
        (row(proj_bias), row(second_gain), row(second_shift), row(expand_bias),
         row(contract_bias), row(first_gain)),
    )
    pairs = heads // PAIR
    if not fuse:
        scatter = partial(lax.psum_scatter, axis_name="dp", scatter_dimension=1, tiled=True)
        ff = scatter(ff.reshape(ff.shape[0], width, ff.shape[-1]))
        pq = scatter(pq.reshape(pq.shape[0], width, pq.shape[-1]))
        small = lax.psum(small, "dp")
    mine = ff.shape[1]
    contract = ff[:, :, :CHUNK].transpose(0, 2, 1).reshape(-1, mine)
    expand = ff[:, :, CHUNK:].transpose(1, 0, 2).reshape(mine, -1)
    proj = pq[0].T
    qkv = pq[1:].reshape(pairs, mine, 3, PAIR).transpose(2, 1, 0, 3).reshape(3, mine, heads)
    rope = small[11:13, :heads].reshape(2, heads // HALF, 2, HALF // 2).sum(2)
    return (
        mixed, pgrad, qkv, proj, expand, contract,
        small[6], small[7], small[8:11, :heads], rope, small[3], small[1], small[2],
        small[4:6].reshape(-1), small[0],
    )


def solution(mesh):
    in_specs = (
        P("dp", None), P("dp", None), P("dp", None), P(), P(), P(None, None, "head"),
        P(None, "head"), P(None, "head", None), P("head", None), P(), P(), P(),
        P(None, "head"), P("head"), P("head", None), P(),
    )
    out_specs = (
        P("dp", None), P("dp", None), P(None, "dp", "head"), P("head", "dp"), P("dp", "head"),
        P("head", "dp"), P(), P(), P(None, "head"), P(None, "head", None), P(), P(), P(),
        P("head"), P(),
    )
    parts = mesh.shape["dp"]
    run = partial(body, parts == PARTS, parts)
    return jax.shard_map(run, mesh=mesh, in_specs=in_specs, out_specs=out_specs, check_vma=False)
```

time: 1090 us -> 235 us (0.22)
  waiting for transfers between devices: 587 us -> 0 us
  Pallas kernels: 0 us -> 201 us
  matrix products: 180 us -> 0 us
  other arithmetic: 121 us -> 0.87 us
  blocking collectives: 79.5 us -> 0 us
  local copies, waits for them, and re-layouts: 93.3 us -> 30.9 us
  between operations: 15.7 us -> 0.73 us
    reduce_scatter x3 -> x0, waiting for transfers between devices: 415 us -> none  [the longest x1 144 us: body(): lax.psum_scatter(expand_grad, 'dp', scatter_dimension=0, tiled=True)]
    pallas_call x0 -> x2, Pallas kernels: none -> 201 us  [the longest x1 171 us: main_call(): pl.pallas_call(partial(main_kernel, fuse, pairs, chunks), name='main', ou...]
    dot_general x34 -> x0, matrix products: 180 us -> none  [the longest x6 27.3 us: one_block(): jnp.einsum('qhd,khd->hqk', query_block, key_heads, preferred_element_type...]
    psum x5 -> x0, waiting for transfers between devices: 99.8 us -> none  [the longest x2 50.6 us: run_forward(): lax.psum(jnp.dot(attended_low, weight_proj, preferred_element_type=jnp.fl...]
    psum x1 -> x0, blocking collectives: 79.5 us -> none  [body(): lax.psum((first_gain_grad, first_shift_grad, qkv_bias_grad, rope_freqs_gr...]
    unnamed x10 -> x0, waiting for transfers between devices: 72.7 us -> none
    sub x3 -> x0, other arithmetic: 34.2 us -> none  [the longest x2 33.5 us: one_block(): exp_scores = jnp.exp(scores - row_max)]
    dynamic_update_slice x4 -> x0, local copies, waits for them, and re-layouts: 33.3 us -> none  [attend_forward(): block_outs, log_sum = lax.map(one_block, (query_blocks, segment_blocks))]
  transfers between devices with their start and end apart: 9 -> 0, of which waited for: 8 -> 0; matrix products, arithmetic and copies ran while one was open for 5% -> 0% of each run, Pallas kernels for 0% -> 0%
where the time goes in v1:
time: 235 us; the launch traced here: 234 us
  Pallas kernels  201 us (86%)
  local copies, waits for them, and re-layouts  30.9 us (13%)
    pallas_call x1, Pallas kernels, main_call(): pl.pallas_call(partial(main_kernel, fuse, pairs, chunks), name='main', ou...  171 us
    pallas_call x1, Pallas kernels, front(): pl.pallas_call(front_kernel, name='front', out_shape=outs, in_specs=[pl.B...  30.3 us
    unnamed x31, local copies, waits for them, and re-layouts  13 us
    reshape x7, local copies, waits for them, and re-layouts, body(): row = lambda v: v.reshape(1, -1)  7.74 us

profile of v1, /device:TPU:0, one launch (start us, length us, event | category | flops | bytes accessed | tf_op | source)
XLA Modules:
  0.0 233.8 jit_solution(6464094015297318455)
XLA Ops:
  2.0 1.3 reshape.76.bias_p
  3.3 1.3 reshape.77.gain_two
  4.6 1.3 reshape.78.shift_two
  5.8 1.3 reshape.80.bias_c
  7.1 0.8 copy.40.grids
  7.9 0.8 pad_maximum_fusion
  8.8 1.3 reshape.79.bias_e
  10.8 30.3 %front.1 = (bf16[1024,384]{1,0:T(8,128)(2,1)S(1)}, bf16[1024,384]{1,0:T(8,128)(2,1)S(1)}, bf16[1024,384]{1,0:T(8,128)(2,1)S(1)}, bf16[1024,768]{1,0:T(8,128)(2,1...) custom-call(s32[6,2]{1,0:T(8,128)S(1)} %copy.40.grids, ...), custom_call_target="tpu_custom_call" | custom-call | tf_op jit(solution)/shard_map/front/pallas_call | solution.py:189
  41.1 1.2 copy-done
  42.2 0.9 copy-done.1
  43.2 1.0 copy-done.2
  44.1 0.9 copy-done.3
  45.0 0.8 copy-done.4
  47.8 170.9 %main.1 = (bf16[1024,768]{1,0:T(8,128)(2,1)}, f32[1024,768]{1,0:T(8,128)}, f32[6,48,512]{2,1,0:T(8,128)}, f32[4,48,384]{2,1,0:T(8,128)}, f32[16,768]{1,0:T(8,128)}) custom-call(f32[1024,384]{1,0:T(8,128)} %get-tuple-element.31.att_h, bf16[1024,384]{1,0:T(8,128)(2,1)} %copy-done.1, bf16[1024,384]{1,0:T(8,128)(2,1)} %copy-done.2, bf16[1024,384]{1,0:T(8,128)(2,1)} %copy-done.3, ...), custom_call_target="tpu_custom_call" | custom-call | tf_op jit(solution)/shard_map/main/pallas_call | solution.py:756
  218.8 0.8 slice.46
  219.6 1.3 slice.45
  220.9 0.7 slice.50
  221.6 1.6 slice_reduce_fusion
  224.6 1.5 slice_bitcast_fusion.2
  226.1 0.9 slice.39
  227.3 0.8 reshape.82
  229.6 1.1 copy.49
  230.8 1.3 copy-done.10
  232.1 1.7 copy.50
  (33 shorter events, 7.3 us)
Async XLA Ops:
  1.3 39.7 %copy-start.8 = (f32[1,768]{1,0:T(1,128)}, f32[1,768]{1,0:T(1,128)S(1)}, u32[]{:S(2)}) copy-start(f32[1,768]{1,0:T(1,128)S(1)} %reshape.73.gain.gain_one) | copy-start | bytes 9220
  10.1 0.7 copy-start.9
  41.1 1.2 copy-start
  42.2 0.9 copy-start.1
  43.2 1.0 copy-start.2
  44.1 0.9 copy-start.3
  45.0 0.8 copy-start.4
  45.8 0.7 copy-start.5
  46.5 0.7 copy-start.6
  47.2 0.6 copy-start.7
  218.8 9.3 %copy-start.12 = (f32[6,48,512]{2,1,0:T(8,128)S(1)}, f32[6,48,512]{2,1,0:T(8,128)}, u32[]{:S(2)}) copy-start(f32[6,48,512]{2,1,0:T(8,128)} %get-tuple-element.45) | copy-start | bytes 1769476
  227.3 2.4 %copy-start.11 = (bf16[1024,768]{1,0:T(8,128)(2,1)S(1)}, bf16[1024,768]{1,0:T(8,128)(2,1)}, u32[]{:S(2)}) copy-start(bf16[1024,768]{1,0:T(8,128)(2,1)} %get-tuple-element.85) | copy-start | bytes 4718596
  229.6 2.5 %copy-start.10 = (f32[1024,768]{1,0:T(8,128)S(1)}, f32[1024,768]{1,0:T(8,128)}, u32[]{:S(2)}) copy-start(f32[1024,768]{1,0:T(8,128)} %get-tuple-element.86) | copy-start | bytes 9437188

commit v2 on v1

--- a/solution.py
+++ b/solution.py
@@ -68,20 +68,14 @@
     return (lane // HALF == h).astype(F32)
 
 
-def front_kernel(
-    grids, x, gain, shift, w, b, freqs,
-    q8, key, val, nf, att, lse, ohq, ohk, cos, sin, pos,
-    kx, lcol,
-):
-    rows_all = x.shape[0]
-    slots = grids.shape[0]
-    pairs = q8.shape[1] // PAIR
+def front_rows(grids, slots, x, gain, shift, w, b, freqs, q8, key, val, nf, ohq, ohk, cossin, pos):
+    rows_all, width_all = q8.shape
+    pairs = width_all // PAIR
     side = lax.broadcasted_iota(jnp.int32, (32, 1), 0).astype(F32)
-    ang_r = side * freqs[0:1, :]
-    ang_c = side * freqs[1:2, :]
+    ang_r = side * freqs[0]
+    ang_c = side * freqs[1]
     table_r = jnp.concatenate([jnp.cos(ang_r), jnp.sin(ang_r)], axis=1)
     table_c = jnp.concatenate([jnp.cos(ang_c), jnp.sin(ang_c)], axis=1)
-    width_all = q8.shape[1]
 
     def first(r):
         rows = aligned(r, R)
@@ -92,10 +86,10 @@
         end = jnp.int32(0)
         for s in range(slots):
             begin = end
-            end = end + grids[s, 0] * grids[s, 1]
+            end = end + grids[0, s] * grids[1, s]
             inside = (t >= begin) & (t < end)
             start = jnp.where(inside, begin, start)
-            width = jnp.where(inside, grids[s, 1], width)
+            width = jnp.where(inside, grids[1, s], width)
             seg = seg + (t >= end).astype(jnp.int32)
         real = (seg < slots).astype(F32)
         off = (t - start).astype(F32)
@@ -118,28 +112,33 @@
         got_c = jnp.dot(hot_c, table_c, precision=lax.Precision.HIGHEST, preferred_element_type=F32)
         cr, sr = got_r[:, :width_all], got_r[:, width_all:]
         cc, sc = got_c[:, :width_all], got_c[:, width_all:]
-        cos[rows, :] = cr * cc - sr * sc
-        sin[rows, :] = sr * cc + cr * sc
+        cossin[rows, :width_all] = cr * cc - sr * sc
+        cossin[rows, width_all:] = sr * cc + cr * sc
         unit, _ = unit_of(x[rows, :].astype(F32))
-        normed = (unit * gain[...] + shift[...]).astype(BF16)
+        normed = (unit * gain + shift).astype(BF16)
         nf[rows, :] = normed
         lane_first = lane % HALF < HALF // 2
         sign = jnp.where(lane_first, -1.0, 1.0)
         for k, out in ((0, q8), (1, key)):
-            got = dot_nn(normed, w[k]) + b[k : k + 1, :]
+            got = dot_nn(normed, w[:, k * width_all : (k + 1) * width_all]) + b[k : k + 1, :]
             for p in range(pairs):
                 cols = slice(p * PAIR, (p + 1) * PAIR)
                 part = got[:, cols]
-                turned = part * cos[rows, cols] + swap_halves(part, lane_first) * (
-                    sin[rows, cols] * sign
+                turned = part * cossin[rows, cols] + swap_halves(part, lane_first) * (
+                    cossin[rows, width_all + p * PAIR : width_all + (p + 1) * PAIR] * sign
                 )
                 turned = turned.astype(BF16)
                 if k == 0:
                     turned = turned * jnp.asarray(HALF**-0.5, BF16)
                 out[rows, cols] = turned
-        val[rows, :] = (dot_nn(normed, w[2]) + b[2:3, :]).astype(BF16)
+        got = dot_nn(normed, w[:, 2 * width_all : 3 * width_all])
+        val[rows, :] = (got + b[2:3, :]).astype(BF16)
 
     loop(rows_all // R, first)
+
+
+def front_heads(q8, key, val, ohq, ohk, att, lse, kx, lcol):
+    rows_all, width_all = q8.shape
 
     def heads(p):
         cols = aligned(p, PAIR)
@@ -166,7 +165,7 @@
 
             loop(rows_all // R, queries)
 
-    loop(pairs, heads)
+    loop(width_all // PAIR, heads)
 
     def turn(r):
         rows = aligned(r, PAIR)
@@ -175,43 +174,27 @@
     loop(rows_all // PAIR, turn)
 
 
-def front(grids, x, gain, shift, w, b, freqs):
-    rows, width = x.shape
-    cols = w.shape[2]
-    shape = jax.ShapeDtypeStruct
-    vm = pl.BlockSpec(memory_space=pltpu.VMEM)
-    outs = [
-        shape((rows, cols), BF16), shape((rows, cols), BF16), shape((rows, cols), BF16),
-        shape((rows, width), BF16), shape((rows, cols), F32), shape((8, rows), F32),
-        shape((rows, PAIR), BF16), shape((rows, PAIR), BF16),
-        shape((rows, cols), F32), shape((rows, cols), F32), shape((rows, PAIR), F32),
-    ]
-    return pl.pallas_call(
-        front_kernel,
-        name="front",
-        out_shape=outs,
-        in_specs=[pl.BlockSpec(memory_space=pltpu.SMEM)] + [vm] * 6,
-        out_specs=[vm] * len(outs),
-        scratch_shapes=[pltpu.VMEM((rows, PAIR), BF16), pltpu.VMEM((rows, PAIR), F32)],
-        compiler_params=pltpu.CompilerParams(vmem_limit_bytes=48 << 20),
-    )(grids, x, gain, shift, w, b, freqs)
-
-
 PARTS = 16
 
 
 def main_kernel(
     fuse, pairs, chunks,
-    att_h, q8_h, key_h, val_h, nf_h, ohq_h, ohk_h, cos_h, sin_h, lse_h, pos_h,
     x_h, og_h, wp_h, we_h, wc_h, wq_h,
-    bias_p, gain_two, shift_two, bias_e, bias_c, gain_one,
-    mixed_h, pgrad_h, ff_h, pq_h, small_h,
+    grids, freqs, bias_q, *rest,
+):
+    (
+    gain_one, shift_one, bias_p, gain_two, shift_two, bias_e, bias_c,
+    mixed_h, pgrad_h, ff_h, pq_h, small_h, nf_h, cossin_h,
     att, q8, key, val, ohq, ohk, lse, pos, x, cot, wp, we, wc,
     acc_a, acc_b, xbuf, mid, cott, ns, nst, act, hgb, dgrad, delta,
     km, vm, kt, kmt, dk, dv, dqt, qkvg, cos, sin, sums,
     gf, gq, r1, r2, r3, small, small_r,
     lsem, xs, xr, credit, s1, e1, s2, e2, s3, e3, c1, c2, c3, ms, mr, osem,
-):
+    ) = rest
+    gain_one, shift_one, bias_p, gain_two, shift_two, bias_e, bias_c = (
+        v[...].reshape(1, -1)
+        for v in (gain_one, shift_one, bias_p, gain_two, shift_two, bias_e, bias_c)
+    )
     me = lax.axis_index("dp")
     core = lax.axis_index("head")
     blocks = x.shape[0] // R
@@ -233,23 +216,18 @@
         copy.start()
         return copy
 
-    get_att = load(att_h, att, 0)
+    heads = q8.shape[1]
+    slots = grids.shape[1]
+    get_x = load(x_h, x, 4)
+    get_wq = [load(wq_h.at[k], we.at[:, pl.ds(k * heads, heads)], 7 + k) for k in range(3)]
     get_wp = load(wp_h, wp, 1)
     get_og = load(og_h, cot, 2)
-    get_pos = load(pos_h, pos, 3)
-    get_x = load(x_h, x, 4)
-    get_we = load(we_h, we, 5)
     get_wc = load(wc_h, wc, 6)
-    get_late = [
-        load(q8_h, q8, 7), load(key_h, key, 8), load(val_h, val, 9),
-        load(ohq_h, ohq, 10), load(ohk_h, ohk, 11), load(lse_h, lse, 12),
-    ]
 
     barrier = pltpu.get_barrier_semaphore()
     friends = [mate] + ([peer1, peer2] + peers_z if fuse else [])
     for friend in friends:
         pl.semaphore_signal(barrier, inc=1, device_id=friend, device_id_type=MESH)
-    pl.semaphore_wait(barrier, len(friends))
 
     def exchange(src, r):
         return pltpu.make_async_remote_copy(
@@ -392,8 +370,24 @@
 
     small[...] = jnp.zeros_like(small)
     sums[...] = jnp.zeros_like(sums)
-
-    get_att.wait()
+    sums[7:8, :] = bias_e
+
+    get_x.wait()
+    for copy in get_wq:
+        copy.wait()
+    turns = []
+    for axis in range(2):
+        lines = [freqs[n, axis : axis + 1, :] for n in range(heads // HALF) for _ in range(2)]
+        turns.append(jnp.concatenate(lines, axis=1))
+    front_rows(
+        grids, slots, x, gain_one, shift_one, we, bias_q, turns,
+        q8, key, val, ns, ohq, ohk, acc_b, pos,
+    )
+    get_we = load(we_h, we, 5)
+    put_nf = load(ns, nf_h, 10)
+    put_cossin = load(acc_b.at[:, pl.ds(0, 2 * heads)], cossin_h, 11)
+    front_heads(q8, key, val, ohq, ohk, att, lse, km, dk)
+    pl.semaphore_wait(barrier, len(friends))
     get_wp.wait()
 
     def project(r):
@@ -403,7 +397,6 @@
     loop(blocks, project)
 
     get_og.wait()
-    get_pos.wait()
 
     def mask_cot(r):
         rows = aligned(r, R)
@@ -414,18 +407,19 @@
         cott[:, rows] = jnp.transpose(low)
 
     loop(blocks, mask_cot)
-    get_x.wait()
+    put_nf.wait()
+    put_cossin.wait()
 
     def second_norm(r):
         exchange(acc_a, r).wait()
 
         def sub(i):
             rows = pl.ds(pl.multiple_of(r * R + i * SUB, SUB), SUB)
-            middle = x[rows, :].astype(F32) + ((acc_a[rows, :] + xbuf[rows, :]) + bias_p[...])
+            middle = x[rows, :].astype(F32) + ((acc_a[rows, :] + xbuf[rows, :]) + bias_p)
             unit, _ = unit_of(middle)
             mid[rows, :] = middle
-            ns[rows, :] = (unit * gain_two[...] + shift_two[...]).astype(BF16)
-            acc_b[rows, :] = 0.5 * (middle + bias_c[...])
+            ns[rows, :] = (unit * gain_two + shift_two).astype(BF16)
+            acc_b[rows, :] = 0.5 * (middle + bias_c)
             acc_a[rows, :] = jnp.zeros_like(middle)
 
         loop(R // SUB, sub)
@@ -441,7 +435,7 @@
 
         def rows_of(r):
             rows = aligned(r, R)
-            hidden = dot_nn(ns[rows, :], we[:, cols]) + bias_e[:, cols]
+            hidden = dot_nn(ns[rows, :], we[:, cols]) + sums[7:8, cols]
             upstream = dot_nt(cot[rows, :], wc[cols, :])
             phi = 0.5 * (1.0 + lax.erf(hidden * (0.5**0.5)))
             slope = phi + hidden * (jnp.exp(-0.5 * hidden * hidden) * (0.3989422804014327))
@@ -459,6 +453,8 @@
         got = dot_nn(nst[...], hgb[...])
         gf[j, :, :, pl.ds(CHUNK, CHUNK)] = got.reshape(gf.shape[1], gf.shape[2], CHUNK)
         ff.start1(j)
+        if fuse:
+            pl.when(j == 3)(lambda: ff.finish1(0))
 
     loop(chunks, feed)
 
@@ -468,7 +464,6 @@
 
     loop(blocks, send_second)
     get_nf = load(nf_h, ns, 0)
-    ff.finish1(0)
     ff.finish1(1)
 
     def second_back(r):
@@ -480,7 +475,7 @@
             unit, inv = unit_of(mid[rows, :])
             small[0, 1:2, :] = small[0, 1:2, :] + jnp.sum(up * unit, axis=0, keepdims=True)
             small[0, 2:3, :] = small[0, 2:3, :] + jnp.sum(up, axis=0, keepdims=True)
-            grad = cot[rows, :].astype(F32) + norm_back(up, unit, inv, gain_two[...])
+            grad = cot[rows, :].astype(F32) + norm_back(up, unit, inv, gain_two)
             mid[rows, :] = grad
             low = grad.astype(BF16)
             cot[rows, :] = low
@@ -505,8 +500,10 @@
         )
 
     loop(blocks, second_back)
+    ff.finish2(0)
     gq[0] = dot_nn(cott[...], att[...].astype(BF16)).reshape(gq.shape[1:])
     pq.start1(0)
+    ff.finish1(2)
 
     def send_mixed(r):
         take_credit(r)
@@ -523,8 +520,6 @@
     get_wq = [
         load(wq_h.at[k], we.at[:, pl.ds(k * pairs * PAIR, pairs * PAIR)], 4 + k) for k in range(3)
     ]
-    for copy in get_late:
-        copy.wait()
     kt[...] = jnp.transpose(key[...])
 
     def mixed_block(r):
@@ -540,8 +535,8 @@
 
     def pair_back(p):
         cols = aligned(p, PAIR)
-        get_cos = load(cos_h.at[:, cols], cos, 0)
-        get_sin = load(sin_h.at[:, cols], sin, 1)
+        get_cos = load(cossin_h.at[:, cols], cos, 0)
+        get_sin = load(cossin_h.at[:, aligned(pairs + p, PAIR)], sin, 1)
         dk[...] = jnp.zeros_like(dk)
         dv[...] = jnp.zeros_like(dv)
         dqt[...] = jnp.zeros_like(dqt)
@@ -570,10 +565,13 @@
 
             loop(blocks, query_back)
             if fuse:
-                pl.when(n < 4)(lambda: ff.finish1(n + 2))
-                ff.finish2(n)
-
-        loop(2, head_back)
+                if h == 0:
+                    ff.finish2(p + 1)
+                else:
+                    ff.finish1(p + 3)
+
+        head_back(0)
+        head_back(1)
         get_cos.wait()
         get_sin.wait()
 
@@ -613,10 +611,7 @@
         gq[p + 1] = dot_nn(nst[...], qkvg[...]).reshape(gq.shape[1:])
         pq.start1(p + 1)
         if fuse:
-            pl.when(p == 0)(lambda: pq.finish1(0))
-            pl.when(p == 1)(lambda: pq.finish1(1))
-            ff.finish3(p * 2)
-            ff.finish3(p * 2 + 1)
+            ff.finish3(p)
 
     loop(pairs, pair_back)
 
@@ -647,19 +642,23 @@
     copy = small_copy(0, 0, mate)
     copy.start()
     if fuse:
-        pq.finish2(0)
+        ff.finish2(4)
+        pq.finish1(0)
+        ff.finish3(3)
     copy.wait()
     line = lax.broadcasted_iota(jnp.int32, small.shape[1:], 0)
     small[1] = small[0] + jnp.where((line == 6) | (line == 7), small_r[0], 0.0)
     if fuse:
         copy = small_copy(1, 1, peer1)
         copy.start()
-        pq.finish1(2)
+        ff.finish2(5)
         copy.wait()
         small[2] = small[1] + small_r[1]
         copy = small_copy(2, 2, peer2)
         copy.start()
-        pq.finish2(1)
+        pq.finish1(1)
+        pq.finish2(0)
+        ff.finish3(4)
         copy.wait()
         small[3] = small[2] + small_r[2]
         copies = [small_copy(3 + k, 3, peers_z[k]) for k in range(3)]
@@ -674,7 +673,7 @@
             rows = pl.ds(pl.multiple_of(r * R + i * SUB, SUB), SUB)
             unit, inv = unit_of(x[rows, :].astype(F32))
             up = acc_a[rows, :] + xbuf[rows, :]
-            mid[rows, :] = mid[rows, :] + norm_back(up, unit, inv, gain_one[...])
+            mid[rows, :] = mid[rows, :] + norm_back(up, unit, inv, gain_one)
 
         loop(R // SUB, sub)
         rows = aligned(r, R)
@@ -688,6 +687,9 @@
     out_small = pltpu.make_async_copy(small.at[last], small_h, lsem.at[0])
     out_small.start()
     if fuse:
+        pq.finish1(2)
+        pq.finish2(1)
+        ff.finish3(5)
         pq.finish3(0)
         pq.finish1(3)
         pq.finish2(2)
@@ -707,10 +709,10 @@
     loop(blocks, finish_out)
 
 
-def main_call(fuse, parts, big, small_in):
-    (att, q8, key, val, nf, ohq, ohk, cos, sin, lse, pos, x, og, wp, we, wc, wq) = big
+def main_call(fuse, parts, big, grids, freqs, bias_q, vectors):
+    x, og, wp, we, wc, wq = big
     rows, width = x.shape
-    heads = q8.shape[1]
+    heads = wq.shape[2]
     hidden = we.shape[1]
     pairs, chunks = heads // PAIR, hidden // CHUNK
     shape = jax.ShapeDtypeStruct
@@ -726,7 +728,8 @@
         slots = 1
     outs = [
         shape((rows, width), BF16), shape((rows, width), F32), shape(ff_shape, F32),
-        shape(pq_shape, F32), shape((16, width), F32),
+        shape(pq_shape, F32), shape((16, width), F32), shape((rows, width), BF16),
+        shape((rows, 2 * heads), F32),
     ]
     any_spec = pl.BlockSpec(memory_space=ANY)
     vm_spec = pl.BlockSpec(memory_space=pltpu.VMEM)
@@ -757,13 +760,95 @@
         partial(main_kernel, fuse, pairs, chunks),
         name="main",
         out_shape=outs,
-        in_specs=[any_spec] * len(big) + [vm_spec] * len(small_in),
+        in_specs=[any_spec] * len(big)
+        + [pl.BlockSpec(memory_space=pltpu.SMEM)]
+        + [vm_spec] * (2 + len(vectors)),
         out_specs=[any_spec] * len(outs),
         scratch_shapes=scratch,
         compiler_params=pltpu.CompilerParams(
             collective_id=0, has_side_effects=True, vmem_limit_bytes=67043328
         ),
-    )(*big, *small_in)
+    )(*big, grids, freqs, bias_q, *vectors)
+
+
+def finish_kernel(
+    mixed_h, pgrad_h, ff_h, pq_h, small_h,
+    mixed_o, pgrad_o, qkv_o, proj_o, expand_o, contract_o,
+    gain_one, shift_one, bias_q, rope, bias_p, gain_two, shift_two, bias_e, bias_c,
+    mixed, pgrad, ff, pq, small, isem, osem,
+):
+    blocks = mixed.shape[0] // R
+    chunks, pairs = ff.shape[0], pq.shape[0] - 1
+    jobs = [(small_h, small, [])]
+    for src, buf, dst in ((pgrad_h, pgrad, pgrad_o), (mixed_h, mixed, mixed_o)):
+        for r in range(blocks):
+            part = (pl.ds(r * R, R), slice(None))
+            jobs.append((src.at[part], buf.at[part], [(buf.at[part], dst.at[part])]))
+    for j in range(chunks):
+        cols = pl.ds(j * CHUNK, CHUNK)
+        jobs.append((ff_h.at[j], ff.at[j], [
+            (ff.at[j, :, pl.ds(0, CHUNK)], contract_o.at[:, cols]),
+            (ff.at[j, :, pl.ds(CHUNK, CHUNK)], expand_o.at[:, cols]),
+        ]))
+    jobs.append((pq_h.at[0], pq.at[0], [(pq.at[0], proj_o)]))
+    for p in range(pairs):
+        jobs.append((pq_h.at[p + 1], pq.at[p + 1], [
+            (pq.at[p + 1, :, pl.ds(k * PAIR, PAIR)], qkv_o.at[k, :, pl.ds(p * PAIR, PAIR)])
+            for k in range(3)
+        ]))
+    gets = [pltpu.make_async_copy(a, b, isem.at[i]) for i, (a, b, _) in enumerate(jobs)]
+    for get in gets:
+        get.start()
+    puts = []
+    for get, (_, _, todo) in zip(gets, jobs):
+        get.wait()
+        for a, b in todo:
+            puts.append(pltpu.make_async_copy(a, b, osem.at[len(puts)]))
+            puts[-1].start()
+    heads = bias_q.shape[1]
+    for k, out in (
+        (6, gain_one), (7, shift_one), (3, bias_p), (1, gain_two), (2, shift_two), (0, bias_c),
+    ):
+        out[...] = small[k, :]
+    half = bias_e.shape[0] // 2
+    bias_e[:half] = small[4, :half]
+    bias_e[half:] = small[5, :half]
+    bias_q[...] = small[8:11, :heads]
+    for p in range(pairs):
+        tile = small[8:16, p * PAIR : (p + 1) * PAIR]
+        both = tile + pltpu.roll(tile, PAIR - HALF // 2, 1)
+        rope[2 * p] = both[3:5, : HALF // 2]
+        rope[2 * p + 1] = pltpu.roll(both, HALF, 1)[3:5, : HALF // 2]
+    for put in puts:
+        put.wait()
+
+
+def finish(mixed, pgrad, ff, pq, small, hidden):
+    rows, width = mixed.shape
+    mine = ff.shape[1]
+    heads = pq.shape[2]
+    shape = lambda *s: jax.ShapeDtypeStruct(s, F32)
+    outs = [
+        jax.ShapeDtypeStruct((rows, width), BF16), shape(rows, width), shape(3, mine, heads),
+        shape(mine, heads), shape(mine, hidden), shape(mine, hidden), shape(width), shape(width),
+        shape(3, heads), shape(heads // HALF, 2, HALF // 2), shape(width), shape(width),
+        shape(width), shape(hidden), shape(width),
+    ]
+    any_spec = pl.BlockSpec(memory_space=ANY)
+    vm_spec = pl.BlockSpec(memory_space=pltpu.VMEM)
+    reads = 1 + 2 * (rows // R) + ff.shape[0] + pq.shape[0]
+    writes = 2 * (rows // R) + 2 * ff.shape[0] + 3 * pq.shape[0] - 2
+    big = (mixed, pgrad, ff, pq, small)
+    return pl.pallas_call(
+        finish_kernel,
+        name="finish",
+        out_shape=outs,
+        in_specs=[any_spec] * 5,
+        out_specs=[any_spec] * 6 + [vm_spec] * (len(outs) - 6),
+        scratch_shapes=[pltpu.VMEM(v.shape, v.dtype) for v in big]
+        + [pltpu.SemaphoreType.DMA((reads,)), pltpu.SemaphoreType.DMA((writes,))],
+        compiler_params=pltpu.CompilerParams(vmem_limit_bytes=67043328),
+    )(*big)
 
 
 def body(
@@ -773,36 +858,27 @@
     contract_weight, contract_bias,
 ):
     width = patches.shape[1]
-    heads = qkv_weight.shape[2]
-    freqs = jnp.concatenate([rope_freqs, rope_freqs], axis=2).reshape(2, heads)
-    row = lambda v: v.reshape(1, -1)
-    q8, key, val, nf, att, lse, ohq, ohk, cos, sin, pos = front(
-        image_grids, patches, row(first_gain), row(first_shift), qkv_weight, qkv_bias, freqs
-    )
-    mixed, pgrad, ff, pq, small = main_call(
+    mixed, pgrad, ff, pq, small, _, _ = main_call(
         fuse,
         parts,
-        (att, q8, key, val, nf, ohq, ohk, cos, sin, lse, pos, patches, out_grad,
-         proj_weight, expand_weight, contract_weight, qkv_weight),
-        (row(proj_bias), row(second_gain), row(second_shift), row(expand_bias),
-         row(contract_bias), row(first_gain)),
+        (patches, out_grad, proj_weight, expand_weight, contract_weight, qkv_weight),
+        image_grids.T,
+        rope_freqs.transpose(1, 0, 2),
+        qkv_bias,
+        (first_gain, first_shift, proj_bias, second_gain, second_shift, expand_bias, contract_bias),
     )
-    pairs = heads // PAIR
     if not fuse:
         scatter = partial(lax.psum_scatter, axis_name="dp", scatter_dimension=1, tiled=True)
         ff = scatter(ff.reshape(ff.shape[0], width, ff.shape[-1]))
         pq = scatter(pq.reshape(pq.shape[0], width, pq.shape[-1]))
         small = lax.psum(small, "dp")
-    mine = ff.shape[1]
-    contract = ff[:, :, :CHUNK].transpose(0, 2, 1).reshape(-1, mine)
-    expand = ff[:, :, CHUNK:].transpose(1, 0, 2).reshape(mine, -1)
-    proj = pq[0].T
-    qkv = pq[1:].reshape(pairs, mine, 3, PAIR).transpose(2, 1, 0, 3).reshape(3, mine, heads)
-    rope = small[11:13, :heads].reshape(2, heads // HALF, 2, HALF // 2).sum(2)
+    (
+        mixed, pgrad, qkv, proj, expand, contract, gain_one, shift_one, bias_q, rope,
+        bias_p, gain_two, shift_two, bias_e, bias_c,
+    ) = finish(mixed, pgrad, ff, pq, small, expand_bias.shape[0])
     return (
-        mixed, pgrad, qkv, proj, expand, contract,
-        small[6], small[7], small[8:11, :heads], rope, small[3], small[1], small[2],
-        small[4:6].reshape(-1), small[0],
+        mixed, pgrad, qkv, proj.T, expand, contract.T, gain_one, shift_one, bias_q,
+        rope.transpose(1, 0, 2), bias_p, gain_two, shift_two, bias_e, bias_c,
     )
 
 

time: 235 us -> 189 us (0.80)
  local copies, waits for them, and re-layouts: 30.9 us -> 0 us
  Pallas kernels: 201 us -> 188 us
    pallas_call x1, Pallas kernels: 30.3 us -> 5.56 us  [finish(): pl.pallas_call(finish_kernel, name='finish', out_shape=outs, in_specs=[an...]
    unnamed x31 -> x0, local copies, waits for them, and re-layouts: 13 us -> none
    pallas_call x1, Pallas kernels: 171 us -> 183 us  [main_call(): pl.pallas_call(partial(main_kernel, fuse, pairs, chunks), name='main', ou...]
    reshape x14 -> x0, local copies, waits for them, and re-layouts: 10.9 us -> none  [the longest x7 7.74 us: body(): row = lambda v: v.reshape(1, -1)]
    slice x5 -> x0, local copies, waits for them, and re-layouts: 5.38 us -> none  [the longest x1 1.62 us: body(): small[0]]
where the time goes in v2:
time: 189 us
  Pallas kernels  188 us (99%)
    pallas_call x1, Pallas kernels, main_call(): pl.pallas_call(partial(main_kernel, fuse, pairs, chunks), name='main', ou...  183 us
    pallas_call x1, Pallas kernels, finish(): pl.pallas_call(finish_kernel, name='finish', out_shape=outs, in_specs=[an...  5.56 us

profile of v2, /device:TPU:0, one launch (start us, length us, event | category | flops | bytes accessed | tf_op | source)
XLA Modules:
  0.0 189.0 jit_solution(18020374542614928510)
XLA Ops:
  0.7 182.7 %main.1 = (bf16[1024,768]{1,0:T(8,128)(2,1)}, f32[1024,768]{1,0:T(8,128)}, f32[6,48,512]{2,1,0:T(8,128)}, f32[4,48,384]{2,1,0:T(8,128)}, f32[16,768]{1,0:T(8,128...) custom-call(bf16[1024,768]{1,0:T(8,128)(2,1)} %x_h.1, bf16[1024,768]{1,0:T(8,128)(2,1)} %og_h.1, ...), custom_call_target="tpu_custom_call" | custom-call | tf_op jit(solution)/shard_map/main/pallas_call | solution.py:759
  183.4 5.6 %finish.1 = (bf16[1024,768]{1,0:T(8,128)(2,1)}, f32[1024,768]{1,0:T(8,128)}, f32[3,48,384]{2,1,0:T(8,128)}, f32[48,384]{1,0:T(8,128)}, f32[48,1536]{1,0:T(8,128)...) custom-call(bf16[1024,768]{1,0:T(8,128)(2,1)} %get-tuple-element.35., ...), custom_call_target="tpu_custom_call" | custom-call | tf_op jit(solution)/shard_map/finish/pallas_call | solution.py:842

commit v3 on v2

--- a/solution.py
+++ b/solution.py
@@ -68,59 +68,73 @@
     return (lane // HALF == h).astype(F32)
 
 
-def front_rows(grids, slots, x, gain, shift, w, b, freqs, q8, key, val, nf, ohq, ohk, cossin, pos):
-    rows_all, width_all = q8.shape
-    pairs = width_all // PAIR
+def pieces(table):
+    high = table.astype(BF16)
+    rest = table - high.astype(F32)
+    mid = rest.astype(BF16)
+    low = (rest - mid.astype(F32)).astype(BF16)
+    return jnp.concatenate([high, mid, low], axis=0)
+
+
+def front_place(grids, slots, freqs, ohq, ohk, cossin, pos):
+    rows_all, width_all = pos.shape[0], freqs[0].shape[1]
     side = lax.broadcasted_iota(jnp.int32, (32, 1), 0).astype(F32)
     ang_r = side * freqs[0]
     ang_c = side * freqs[1]
-    table_r = jnp.concatenate([jnp.cos(ang_r), jnp.sin(ang_r)], axis=1)
-    table_c = jnp.concatenate([jnp.cos(ang_c), jnp.sin(ang_c)], axis=1)
-
-    def first(r):
-        rows = aligned(r, R)
-        t = lax.broadcasted_iota(jnp.int32, (R, 1), 0) + r * R
-        seg = jnp.zeros((R, 1), jnp.int32)
-        start = jnp.zeros((R, 1), jnp.int32)
-        width = jnp.ones((R, 1), jnp.int32)
+    table_r = pieces(jnp.concatenate([jnp.cos(ang_r), jnp.sin(ang_r)], axis=1))
+    table_c = pieces(jnp.concatenate([jnp.cos(ang_c), jnp.sin(ang_c)], axis=1))
+
+    def place(r):
+        rows = aligned(r, 256)
+        t = lax.broadcasted_iota(jnp.int32, (256, 1), 0) + r * 256
+        seg = jnp.zeros((256, 1), jnp.int32)
+        start = jnp.zeros((256, 1), jnp.int32)
+        width = jnp.ones((256, 1), jnp.int32)
         end = jnp.int32(0)
         for s in range(slots):
-            begin = end
+            begun = t >= end
+            start = jnp.where(begun, end, start)
+            width = jnp.where(begun, jnp.maximum(grids[1, s], 1), width)
             end = end + grids[0, s] * grids[1, s]
-            inside = (t >= begin) & (t < end)
-            start = jnp.where(inside, begin, start)
-            width = jnp.where(inside, grids[1, s], width)
-            seg = seg + (t >= end).astype(jnp.int32)
+            seg = jnp.where(t >= end, s + 1, seg)
         real = (seg < slots).astype(F32)
         off = (t - start).astype(F32)
         wide = width.astype(F32)
         grow = jnp.floor((off + 0.5) / wide) * real
         gcol = (off - grow * wide) * real
-        lane = lane_ids(R)
-        pos[rows, :] = (
-            jnp.where(lane == 0, real, 0.0)
-            + jnp.where(lane == 1, grow, 0.0)
-            + jnp.where(lane == 2, gcol, 0.0)
-        )
-        hot = (lane % HALF == seg).astype(F32)
-        ohq[rows, :] = hot.astype(BF16)
-        ohk[rows, :] = ((1.0 - hot) * (-FAR)).astype(BF16)
-        spot = lax.broadcasted_iota(jnp.int32, (R, 32), 1)
-        hot_r = (spot == grow.astype(jnp.int32)).astype(F32)
-        hot_c = (spot == gcol.astype(jnp.int32)).astype(F32)
-        got_r = jnp.dot(hot_r, table_r, precision=lax.Precision.HIGHEST, preferred_element_type=F32)
-        got_c = jnp.dot(hot_c, table_c, precision=lax.Precision.HIGHEST, preferred_element_type=F32)
+        lane = lane_ids(256)
+        pos[rows, :] = jnp.where(lane == 0, real, jnp.where(lane == 1, grow, gcol))
+        hot = lane % HALF == seg
+        ohq[rows, :] = jnp.where(hot, 1.0, 0.0).astype(BF16)
+        ohk[rows, :] = jnp.where(hot, 0.0, -FAR).astype(BF16)
+        spot = (lax.broadcasted_iota(jnp.int32, (256, 96), 1) % 32).astype(F32)
+        got_r = dot_nn(jnp.where(spot == grow, 1.0, 0.0).astype(BF16), table_r)
+        got_c = dot_nn(jnp.where(spot == gcol, 1.0, 0.0).astype(BF16), table_c)
         cr, sr = got_r[:, :width_all], got_r[:, width_all:]
         cc, sc = got_c[:, :width_all], got_c[:, width_all:]
         cossin[rows, :width_all] = cr * cc - sr * sc
         cossin[rows, width_all:] = sr * cc + cr * sc
+
+    loop(rows_all // 256, place)
+
+
+def front_rows(x, gain, shift, w, b, q8, key, val, nf, cossin):
+    rows_all, width_all = q8.shape
+    pairs = width_all // PAIR
+
+    def norm(r):
+        rows = aligned(r, SUB)
         unit, _ = unit_of(x[rows, :].astype(F32))
-        normed = (unit * gain + shift).astype(BF16)
-        nf[rows, :] = normed
-        lane_first = lane % HALF < HALF // 2
+        nf[rows, :] = (unit * gain + shift).astype(BF16)
+
+    loop(rows_all // SUB, norm)
+
+    def project(r):
+        rows = aligned(r, R)
+        lane_first = lane_ids(R) % HALF < HALF // 2
         sign = jnp.where(lane_first, -1.0, 1.0)
         for k, out in ((0, q8), (1, key)):
-            got = dot_nn(normed, w[:, k * width_all : (k + 1) * width_all]) + b[k : k + 1, :]
+            got = dot_nn(nf[rows, :], w[:, k * width_all : (k + 1) * width_all]) + b[k : k + 1, :]
             for p in range(pairs):
                 cols = slice(p * PAIR, (p + 1) * PAIR)
                 part = got[:, cols]
@@ -131,39 +145,55 @@
                 if k == 0:
                     turned = turned * jnp.asarray(HALF**-0.5, BF16)
                 out[rows, cols] = turned
-        got = dot_nn(normed, w[:, 2 * width_all : 3 * width_all])
+        got = dot_nn(nf[rows, :], w[:, 2 * width_all : 3 * width_all])
         val[rows, :] = (got + b[2:3, :]).astype(BF16)
 
-    loop(rows_all // R, first)
-
-
-def front_heads(q8, key, val, ohq, ohk, att, lse, kx, lcol):
+    loop(rows_all // R, project)
+
+
+def front_heads(q8, key, val, ohq, ohk, att, lse, kxs, scs, lcol):
     rows_all, width_all = q8.shape
+    blocks = rows_all // R
+    masks = [head_mask(h).astype(BF16) for h in range(2)]
 
     def heads(p):
         cols = aligned(p, PAIR)
         for h in range(2):
-            mine = head_mask(h).astype(BF16)
-            other = head_mask(1 - h).astype(BF16)
-            kx[...] = key[:, cols] * mine + ohk[...] * other
-
-            def queries(r, h=h, mine=mine, other=other):
-                rows = aligned(r, R)
-                qx = q8[rows, cols] * mine + ohq[rows, :] * other
-                score = dot_nt(qx, kx[...])
-                top = jnp.max(score, axis=-1, keepdims=True)
-                grown = jnp.exp(score - top)
-                total = jnp.sum(grown, axis=-1, keepdims=True)
-                got = dot_nn(grown.astype(BF16), val[:, cols]) * (1.0 / total)
-                lane = lane_ids(R)
-                log_sum = top + jnp.log(total)
-                if h == 0:
-                    att[rows, cols] = got
-                else:
-                    att[rows, cols] = jnp.where(lane < HALF, att[rows, cols], got)
-                lcol[rows, :] = jnp.where(lane == p * 2 + h, log_sum, lcol[rows, :])
-
-            loop(rows_all // R, queries)
+            kxs[h][...] = key[:, cols] * masks[h] + ohk[...] * masks[1 - h]
+
+        def scores(h, r):
+            rows = aligned(r, R)
+            scs[h][...] = dot_nt(q8[rows, cols] * masks[h] + ohq[rows, :] * masks[1 - h], kxs[h][...])
+
+        def weigh(h, r):
+            rows = aligned(r, R)
+            top = jnp.max(scs[h][...], axis=-1, keepdims=True)
+            total = jnp.zeros((R, PAIR), F32)
+            got = jnp.zeros((R, PAIR), F32)
+            for k in range(rows_all // R):
+                keys = slice(k * R, (k + 1) * R)
+                grown = jnp.exp(scs[h][:, keys] - top)
+                for m in range(R // PAIR):
+                    total = total + grown[:, m * PAIR : (m + 1) * PAIR]
+                got = got + dot_nn(grown.astype(BF16), val[keys, cols])
+            total = jnp.sum(total, axis=-1, keepdims=True)
+            got = got * (1.0 / total)
+            lane = lane_ids(R)
+            if h == 0:
+                att[rows, cols] = got
+            else:
+                att[rows, cols] = jnp.where(lane < HALF, att[rows, cols], got)
+            lcol[rows, :] = jnp.where(lane == p * 2 + h, top + jnp.log(total), lcol[rows, :])
+
+        scores(0, 0)
+
+        def step(r):
+            scores(1, r)
+            weigh(0, r)
+            scores(0, jnp.minimum(r + 1, blocks - 1))
+            weigh(1, r)
+
+        loop(blocks, step)
 
     loop(width_all // PAIR, heads)
 
@@ -188,8 +218,8 @@
     att, q8, key, val, ohq, ohk, lse, pos, x, cot, wp, we, wc,
     acc_a, acc_b, xbuf, mid, cott, ns, nst, act, hgb, dgrad, delta,
     km, vm, kt, kmt, dk, dv, dqt, qkvg, cos, sin, sums,
-    gf, gq, r1, r2, r3, small, small_r,
-    lsem, xs, xr, credit, s1, e1, s2, e2, s3, e3, c1, c2, c3, ms, mr, osem,
+    gf, gq, r1, r2, r3, small, small_r, sc0, sc1,
+    lsem, xs, xr, credit, s1, e1, s2, e2, s3, e3, c1, c2, c3, ms, mr, osem, zs,
     ) = rest
     gain_one, shift_one, bias_p, gain_two, shift_two, bias_e, bias_c = (
         v[...].reshape(1, -1)
@@ -346,6 +376,77 @@
                 remote(src, dst, ss.at[self.base + j], rs.at[self.base + j], peer).wait_send()
             pltpu.make_async_copy(self.g.at[j, me], self.out.at[j], osem.at[self.base + j]).wait()
 
+    class Deep:
+        def __init__(self, grads, j, out):
+            self.g, self.j, self.out = grads, j, out
+
+        def quarter(self, k):
+            j = self.j
+            src = self.g.at[j, pl.ds(((zz + k + 1) % 4) * 4, 4)]
+            if k < 2:
+                return remote(src, r1.at[j, pl.ds(4 * k, 4)], s1.at[j], e1.at[j], peers_z[k])
+            return remote(src, r2.at[j], s2.at[j], e2.at[j], peers_z[k])
+
+        def two(self):
+            j = self.j
+            return remote(self.g.at[j, pl.ds(0, 8)], r1.at[j], s1.at[j], e1.at[j], peers_z[0])
+
+        def halves(self):
+            j = self.j
+            return remote(
+                self.g.at[j, pl.ds(0, 2)], r3.at[j, pl.ds(0, 2)], s3.at[j], e3.at[j], peer1
+            )
+
+        def last(self):
+            return remote(
+                self.g.at[self.j, where(zz, fst, 1 - snd)], r3.at[self.j, 2], zs.at[0], zs.at[1],
+                peer2,
+            )
+
+        def result(self):
+            return pltpu.make_async_copy(
+                self.g.at[self.j, me], self.out.at[self.j], osem.at[self.j]
+            )
+
+        def start(self):
+            for k in range(3):
+                self.quarter(k).start()
+
+        def finish1(self):
+            j = self.j
+            self.two().wait_recv()
+            self.quarter(2).wait_recv()
+
+            def one(i):
+                b = zz * 4 + i
+                self.g[j, b] = self.g[j, b] + r1[j, i] + r1[j, 4 + i] + r2[j, i]
+
+            loop(4, one)
+            for s in range(2):
+                remote(
+                    self.g.at[j, where(zz, 1 - fst, s)], r3.at[j, s], s3.at[j], e3.at[j], peer1
+                ).start()
+
+        def finish2(self):
+            j = self.j
+            self.halves().wait_recv()
+            for s in range(2):
+                b = where(zz, fst, s)
+                self.g[j, b] = self.g[j, b] + r3[j, s]
+            self.last().start()
+
+        def finish3(self):
+            self.last().wait_recv()
+            self.g[self.j, me] = self.g[self.j, me] + r3[self.j, 2]
+            self.result().start()
+
+        def drain(self):
+            self.two().wait_send()
+            self.quarter(2).wait_send()
+            self.halves().wait_send()
+            self.last().wait_send()
+            self.result().wait()
+
     class Plain:
         def __init__(self, grads, base, width, out, guard):
             self.g, self.base, self.out = grads, base, out
@@ -367,26 +468,25 @@
     kind = Line if fuse else Plain
     ff = kind(gf, 0, 2 * CHUNK, ff_h, "give")
     pq = kind(gq, chunks, 3 * PAIR, pq_h, "take")
+    deep = Deep(gf, chunks - 1, ff_h)
 
     small[...] = jnp.zeros_like(small)
     sums[...] = jnp.zeros_like(sums)
     sums[7:8, :] = bias_e
 
-    get_x.wait()
-    for copy in get_wq:
-        copy.wait()
     turns = []
     for axis in range(2):
         lines = [freqs[n, axis : axis + 1, :] for n in range(heads // HALF) for _ in range(2)]
         turns.append(jnp.concatenate(lines, axis=1))
-    front_rows(
-        grids, slots, x, gain_one, shift_one, we, bias_q, turns,
-        q8, key, val, ns, ohq, ohk, acc_b, pos,
-    )
+    front_place(grids, slots, turns, ohq, ohk, acc_b, pos)
+    get_x.wait()
+    for copy in get_wq:
+        copy.wait()
+    front_rows(x, gain_one, shift_one, we, bias_q, q8, key, val, ns, acc_b)
     get_we = load(we_h, we, 5)
     put_nf = load(ns, nf_h, 10)
     put_cossin = load(acc_b.at[:, pl.ds(0, 2 * heads)], cossin_h, 11)
-    front_heads(q8, key, val, ohq, ohk, att, lse, km, dk)
+    front_heads(q8, key, val, ohq, ohk, att, lse, (km, vm), (sc0, sc1), dk)
     pl.semaphore_wait(barrier, len(friends))
     get_wp.wait()
 
@@ -430,7 +530,8 @@
     get_we.wait()
     get_wc.wait()
 
-    def feed(j):
+    def feed(i):
+        j = (i + chunks - 1) % chunks
         cols = aligned(j, CHUNK)
 
         def rows_of(r):
@@ -452,9 +553,12 @@
         gf[j, :, :, pl.ds(0, CHUNK)] = got.reshape(gf.shape[1], gf.shape[2], CHUNK)
         got = dot_nn(nst[...], hgb[...])
         gf[j, :, :, pl.ds(CHUNK, CHUNK)] = got.reshape(gf.shape[1], gf.shape[2], CHUNK)
-        ff.start1(j)
         if fuse:
-            pl.when(j == 3)(lambda: ff.finish1(0))
+            pl.when(i == 0)(deep.start)
+            pl.when(i > 0)(lambda: ff.start1(j))
+            pl.when(i == 4)(lambda: ff.finish1(0))
+        else:
+            ff.start1(j)
 
     loop(chunks, feed)
 
@@ -503,7 +607,6 @@
     ff.finish2(0)
     gq[0] = dot_nn(cott[...], att[...].astype(BF16)).reshape(gq.shape[1:])
     pq.start1(0)
-    ff.finish1(2)
 
     def send_mixed(r):
         take_credit(r)
@@ -566,9 +669,11 @@
             loop(blocks, query_back)
             if fuse:
                 if h == 0:
+                    ff.finish1(p + 2)
                     ff.finish2(p + 1)
                 else:
-                    ff.finish1(p + 3)
+                    pl.when(p == 0)(deep.finish1)
+                    pl.when(p > 0)(lambda: ff.finish3(p - 1))
 
         head_back(0)
         head_back(1)
@@ -610,8 +715,6 @@
         loop(blocks, turn_back)
         gq[p + 1] = dot_nn(nst[...], qkvg[...]).reshape(gq.shape[1:])
         pq.start1(p + 1)
-        if fuse:
-            ff.finish3(p)
 
     loop(pairs, pair_back)
 
@@ -642,28 +745,15 @@
     copy = small_copy(0, 0, mate)
     copy.start()
     if fuse:
+        pq.finish1(0)
+        deep.finish2()
         ff.finish2(4)
-        pq.finish1(0)
-        ff.finish3(3)
+        ff.finish3(2)
     copy.wait()
     line = lax.broadcasted_iota(jnp.int32, small.shape[1:], 0)
     small[1] = small[0] + jnp.where((line == 6) | (line == 7), small_r[0], 0.0)
     if fuse:
-        copy = small_copy(1, 1, peer1)
-        copy.start()
-        ff.finish2(5)
-        copy.wait()
-        small[2] = small[1] + small_r[1]
-        copy = small_copy(2, 2, peer2)
-        copy.start()
-        pq.finish1(1)
-        pq.finish2(0)
-        ff.finish3(4)
-        copy.wait()
-        small[3] = small[2] + small_r[2]
-        copies = [small_copy(3 + k, 3, peers_z[k]) for k in range(3)]
-        for copy in copies:
-            copy.start()
+        small_copy(1, 1, peer1).start()
     last = 4 if fuse else 1
 
     def first_back(r):
@@ -681,23 +771,38 @@
 
     loop(blocks, first_back)
     if fuse:
+        pq.finish1(1)
+        pq.finish2(0)
+        ff.finish3(3)
+        pq.finish1(2)
+        pq.finish2(1)
+        ff.finish3(4)
+        deep.finish3()
+        pq.finish3(0)
+        pq.finish1(3)
+        small_copy(1, 1, peer1).wait()
+        small[2] = small[1] + small_r[1]
+        small_copy(2, 2, peer2).start()
+        pq.finish2(2)
+        pq.finish3(1)
+        small_copy(2, 2, peer2).wait()
+        small[3] = small[2] + small_r[2]
+        copies = [small_copy(3 + k, 3, peers_z[k]) for k in range(3)]
+        for copy in copies:
+            copy.start()
+        pq.finish2(3)
+        pq.finish3(2)
         for copy in copies:
             copy.wait()
         small[4] = small[3] + (small_r[3] + small_r[4] + small_r[5])
     out_small = pltpu.make_async_copy(small.at[last], small_h, lsem.at[0])
     out_small.start()
     if fuse:
-        pq.finish1(2)
-        pq.finish2(1)
-        ff.finish3(5)
-        pq.finish3(0)
-        pq.finish1(3)
-        pq.finish2(2)
-        pq.finish3(1)
-        pq.finish2(3)
-        pq.finish3(2)
         pq.finish3(3)
-    loop(chunks, ff.drain)
+        deep.drain()
+        loop(chunks - 1, ff.drain)
+    else:
+        loop(chunks, ff.drain)
     loop(pairs + 1, pq.drain)
     out_small.wait()
 
@@ -752,9 +857,10 @@
         V((rows, PAIR), F32), V((rows, PAIR), F32), V((8, hidden), F32),
         V((chunks, *grain, 2 * CHUNK), F32), V((pairs + 1, *grain, 3 * PAIR), F32),
         recv(8), recv(4), recv(3), V((5, 16, width), F32), V((6, 16, width), F32),
+        V((R, rows), F32), V((R, rows), F32),
         DMA((16,)), DMA((blocks,)), DMA((blocks,)), REG((blocks,)),
         DMA((lines,)), DMA((lines,)), DMA((lines,)), DMA((lines,)), DMA((lines,)), DMA((lines,)),
-        REG((4,)), REG((4,)), REG((4,)), DMA((10,)), DMA((6,)), DMA((lines,)),
+        REG((4,)), REG((4,)), REG((4,)), DMA((10,)), DMA((6,)), DMA((lines,)), DMA((2,)),
     ]
     return pl.pallas_call(
         partial(main_kernel, fuse, pairs, chunks),

time: 189 us -> 171 us (0.905)
  Pallas kernels: 188 us -> 170 us
    pallas_call x1, Pallas kernels: 183 us -> 165 us  [main_call(): pl.pallas_call(partial(main_kernel, fuse, pairs, chunks), name='main', ou...]
where the time goes in v3:
time: 171 us
  Pallas kernels  170 us (99%)
    pallas_call x1, Pallas kernels, main_call(): pl.pallas_call(partial(main_kernel, fuse, pairs, chunks), name='main', ou...  165 us
    pallas_call x1, Pallas kernels, finish(): pl.pallas_call(finish_kernel, name='finish', out_shape=outs, in_specs=[an...  5.56 us

profile of v3, /device:TPU:0, one launch (start us, length us, event | category | flops | bytes accessed | tf_op | source)
XLA Modules:
  0.0 170.7 jit_solution(15255657070205856886)
XLA Ops:
  0.7 164.5 %main.1 = (bf16[1024,768]{1,0:T(8,128)(2,1)}, f32[1024,768]{1,0:T(8,128)}, f32[6,48,512]{2,1,0:T(8,128)}, f32[4,48,384]{2,1,0:T(8,128)}, f32[16,768]{1,0:T(8,128...) custom-call(bf16[1024,768]{1,0:T(8,128)(2,1)} %x_h.1, bf16[1024,768]{1,0:T(8,128)(2,1)} %og_h.1, ...), custom_call_target="tpu_custom_call" | custom-call | tf_op jit(solution)/shard_map/main/pallas_call | solution.py:865
  165.2 5.6 %finish.1 = (bf16[1024,768]{1,0:T(8,128)(2,1)}, f32[1024,768]{1,0:T(8,128)}, f32[3,48,384]{2,1,0:T(8,128)}, f32[48,384]{1,0:T(8,128)}, f32[48,1536]{1,0:T(8,128)...) custom-call(bf16[1024,768]{1,0:T(8,128)(2,1)} %get-tuple-element.35., ...), custom_call_target="tpu_custom_call" | custom-call | tf_op jit(solution)/shard_map/finish/pallas_call | solution.py:948

commit v4 on v3

--- a/solution.py
+++ b/solution.py
@@ -12,6 +12,7 @@
 EPS = 1e-06
 FAR = 2.0**100
 R = 256
+QR = 512
 SUB = 64
 PAIR = 128
 HALF = 64
@@ -151,10 +152,14 @@
     loop(rows_all // R, project)
 
 
-def front_heads(q8, key, val, ohq, ohk, att, lse, kxs, scs, lcol):
+def front_heads(q8, key, val, ohq, ohk, att, kxs, scs, lcol):
     rows_all, width_all = q8.shape
-    blocks = rows_all // R
+    blocks, pieces_all, wide = rows_all // QR, rows_all // R, scs[0].shape[1] // R
     masks = [head_mask(h).astype(BF16) for h in range(2)]
+
+    def piece(h, k):
+        at = (k // wide) * QR
+        return scs[h].at[at : at + QR, (k % wide) * R : (k % wide + 1) * R]
 
     def heads(p):
         cols = aligned(p, PAIR)
@@ -162,23 +167,27 @@
             kxs[h][...] = key[:, cols] * masks[h] + ohk[...] * masks[1 - h]
 
         def scores(h, r):
-            rows = aligned(r, R)
-            scs[h][...] = dot_nt(q8[rows, cols] * masks[h] + ohq[rows, :] * masks[1 - h], kxs[h][...])
+            rows = aligned(r, QR)
+            qx = q8[rows, cols] * masks[h] + ohq[rows, :] * masks[1 - h]
+            for k in range(pieces_all):
+                piece(h, k)[...] = dot_nt(qx, kxs[h][k * R : (k + 1) * R, :])
 
         def weigh(h, r):
-            rows = aligned(r, R)
-            top = jnp.max(scs[h][...], axis=-1, keepdims=True)
-            total = jnp.zeros((R, PAIR), F32)
-            got = jnp.zeros((R, PAIR), F32)
-            for k in range(rows_all // R):
-                keys = slice(k * R, (k + 1) * R)
-                grown = jnp.exp(scs[h][:, keys] - top)
+            rows = aligned(r, QR)
+            top = piece(h, 0)[...]
+            for k in range(1, pieces_all):
+                top = jnp.maximum(top, piece(h, k)[...])
+            top = jnp.max(top, axis=-1, keepdims=True)
+            total = jnp.zeros((QR, PAIR), F32)
+            got = jnp.zeros((QR, PAIR), F32)
+            for k in range(pieces_all):
+                grown = jnp.exp(piece(h, k)[...] - top)
                 for m in range(R // PAIR):
                     total = total + grown[:, m * PAIR : (m + 1) * PAIR]
-                got = got + dot_nn(grown.astype(BF16), val[keys, cols])
+                got = got + dot_nn(grown.astype(BF16), val[k * R : (k + 1) * R, cols])
             total = jnp.sum(total, axis=-1, keepdims=True)
             got = got * (1.0 / total)
-            lane = lane_ids(R)
+            lane = lane_ids(QR)
             if h == 0:
                 att[rows, cols] = got
             else:
@@ -196,12 +205,6 @@
         loop(blocks, step)
 
     loop(width_all // PAIR, heads)
-
-    def turn(r):
-        rows = aligned(r, PAIR)
-        lse[:, rows] = jnp.transpose(lcol[rows, :])[: lse.shape[0], :]
-
-    loop(rows_all // PAIR, turn)
 
 
 PARTS = 16
@@ -218,7 +221,7 @@
     att, q8, key, val, ohq, ohk, lse, pos, x, cot, wp, we, wc,
     acc_a, acc_b, xbuf, mid, cott, ns, nst, act, hgb, dgrad, delta,
     km, vm, kt, kmt, dk, dv, dqt, qkvg, cos, sin, sums,
-    gf, gq, r1, r2, r3, small, small_r, sc0, sc1,
+    gf, gq, r1, r2, r3, small, small_r,
     lsem, xs, xr, credit, s1, e1, s2, e2, s3, e3, c1, c2, c3, ms, mr, osem, zs,
     ) = rest
     gain_one, shift_one, bias_p, gain_two, shift_two, bias_e, bias_c = (
@@ -280,26 +283,40 @@
         )
 
     class Line:
-        def __init__(self, grads, base, width, out, guard):
-            self.g, self.base, self.n, self.out, self.guard = grads, base, width, out, guard
-
-        def buf(self, buf, j, b):
-            return buf.at[j, b, :, pl.ds(0, self.n)]
-
-        def whole(self, buf, j):
-            return buf.at[j, :, :, pl.ds(0, self.n)]
+        def __init__(self, grads, base, width, out, guard, parts):
+            self.g, self.base, self.out, self.guard = grads, base, out, guard
+            self.n, self.parts = width // parts, parts
+
+        def cols(self, k):
+            return pl.ds(k * self.n, self.n)
+
+        def at(self, j, k):
+            return self.base + j * self.parts + k
+
+        def step(self, j, k, first, src, dst, ss, rs, peer):
+            i = self.at(j, k)
+            return remote(
+                self.g.at[j, src, :, self.cols(k)], first.at[j, dst, :, self.cols(k)],
+                ss.at[i], rs.at[i], peer,
+            )
+
+        def whole(self, j, k, n, ss, rs, buf, peer):
+            return self.step(j, k, buf, pl.ds(0, n), pl.ds(0, n), ss, rs, peer)
+
+        def add(self, j, k, b, got):
+            c = self.cols(k)
+            self.g[j, b, :, c] = self.g[j, b, :, c] + got
 
         def start1(self, j):
             if self.guard == "take":
                 pl.semaphore_wait(c1.at[j], 1)
-
-            def one(i):
-                remote(
-                    self.g.at[j, where(i // 2, 1 - fst, i % 2)], self.buf(r1, j, i),
-                    s1.at[self.base + j], e1.at[self.base + j], peer1,
-                ).start()
-
-            loop(8, one)
+            for k in range(self.parts):
+
+                def one(i, k=k):
+                    b = where(i // 2, 1 - fst, i % 2)
+                    self.step(j, k, r1, b, i, s1, e1, peer1).start()
+
+                loop(8, one)
 
         def give(self, sem, j, peers):
             if self.guard == "give":
@@ -312,69 +329,57 @@
                 else:
                     pl.when(j < 4)(go)
 
-        def finish1(self, j):
-            remote(
-                self.g.at[j, pl.ds(0, 8)], self.whole(r1, j),
-                s1.at[self.base + j], e1.at[self.base + j], peer1,
-            ).wait_recv()
+        def finish1(self, j, k=0):
+            self.whole(j, k, 8, s1, e1, r1, peer1).wait_recv()
+            c = self.cols(k)
 
             def one(i):
-                b = where(i // 2, fst, i % 2)
-                self.g[j, b] = self.g[j, b] + self.buf(r1, j, i)[...]
+                self.add(j, k, where(i // 2, fst, i % 2), r1[j, i, :, c])
 
             loop(8, one)
             self.give(c1, j, [peer1])
-            if self.guard == "take":
+            if self.guard == "take" and k == 0:
                 pl.semaphore_wait(c2.at[j], 1)
 
             def two(i):
-                remote(
-                    self.g.at[j, where(i, fst, 1 - snd)], self.buf(r2, j, i),
-                    s2.at[self.base + j], e2.at[self.base + j], peer2,
-                ).start()
+                self.step(j, k, r2, where(i, fst, 1 - snd), i, s2, e2, peer2).start()
 
             loop(4, two)
 
-        def finish2(self, j):
-            remote(
-                self.g.at[j, pl.ds(0, 4)], self.whole(r2, j),
-                s2.at[self.base + j], e2.at[self.base + j], peer2,
-            ).wait_recv()
+        def finish2(self, j, k=0):
+            self.whole(j, k, 4, s2, e2, r2, peer2).wait_recv()
+            c = self.cols(k)
 
             def one(i):
-                b = where(i, fst, snd)
-                self.g[j, b] = self.g[j, b] + self.buf(r2, j, i)[...]
+                self.add(j, k, where(i, fst, snd), r2[j, i, :, c])
 
             loop(4, one)
             self.give(c2, j, [peer2])
-            if self.guard == "take":
+            if self.guard == "take" and k == 0:
                 pl.semaphore_wait(c3.at[j], 3)
-            for k in range(3):
-                remote(
-                    self.g.at[j, where((zz + k + 1) % 4, fst, snd)], self.buf(r3, j, k),
-                    s3.at[self.base + j], e3.at[self.base + j], peers_z[k],
-                ).start()
-
-        def finish3(self, j):
-            remote(
-                self.g.at[j, pl.ds(0, 3)], self.whole(r3, j),
-                s3.at[self.base + j], e3.at[self.base + j], peers_z[0],
-            ).wait_recv()
-            self.g[j, me] = (
-                self.g[j, me]
-                + self.buf(r3, j, 0)[...] + self.buf(r3, j, 1)[...] + self.buf(r3, j, 2)[...]
+            for m in range(3):
+                b = where((zz + m + 1) % 4, fst, snd)
+                self.step(j, k, r3, b, m, s3, e3, peers_z[m]).start()
+
+        def result(self, j, k):
+            c = self.cols(k)
+            return pltpu.make_async_copy(
+                self.g.at[j, me, :, c], self.out.at[j, :, c], osem.at[self.at(j, k)]
             )
+
+        def finish3(self, j, k=0):
+            self.whole(j, k, 3, s3, e3, r3, peers_z[0]).wait_recv()
+            c = self.cols(k)
+            self.add(j, k, me, r3[j, 0, :, c] + r3[j, 1, :, c] + r3[j, 2, :, c])
             self.give(c3, j, peers_z)
-            pltpu.make_async_copy(self.g.at[j, me], self.out.at[j], osem.at[self.base + j]).start()
+            self.result(j, k).start()
 
         def drain(self, j):
-            for src, dst, ss, rs, peer in (
-                (self.g.at[j, pl.ds(0, 8)], self.whole(r1, j), s1, e1, peer1),
-                (self.g.at[j, pl.ds(0, 4)], self.whole(r2, j), s2, e2, peer2),
-                (self.g.at[j, pl.ds(0, 3)], self.whole(r3, j), s3, e3, peers_z[0]),
-            ):
-                remote(src, dst, ss.at[self.base + j], rs.at[self.base + j], peer).wait_send()
-            pltpu.make_async_copy(self.g.at[j, me], self.out.at[j], osem.at[self.base + j]).wait()
+            for k in range(self.parts):
+                self.whole(j, k, 8, s1, e1, r1, peer1).wait_send()
+                self.whole(j, k, 4, s2, e2, r2, peer2).wait_send()
+                self.whole(j, k, 3, s3, e3, r3, peers_z[0]).wait_send()
+                self.result(j, k).wait()
 
     class Deep:
         def __init__(self, grads, j, out):
@@ -448,7 +453,7 @@
             self.result().wait()
 
     class Plain:
-        def __init__(self, grads, base, width, out, guard):
+        def __init__(self, grads, base, width, out, guard, parts):
             self.g, self.base, self.out = grads, base, out
 
         def copy(self, j):
@@ -466,8 +471,8 @@
             self.copy(j).wait()
 
     kind = Line if fuse else Plain
-    ff = kind(gf, 0, 2 * CHUNK, ff_h, "give")
-    pq = kind(gq, chunks, 3 * PAIR, pq_h, "take")
+    ff = kind(gf, 0, 2 * CHUNK, ff_h, "give", 1)
+    pq = kind(gq, chunks, 3 * PAIR, pq_h, "take", 3)
     deep = Deep(gf, chunks - 1, ff_h)
 
     small[...] = jnp.zeros_like(small)
@@ -486,7 +491,7 @@
     get_we = load(we_h, we, 5)
     put_nf = load(ns, nf_h, 10)
     put_cossin = load(acc_b.at[:, pl.ds(0, 2 * heads)], cossin_h, 11)
-    front_heads(q8, key, val, ohq, ohk, att, lse, (km, vm), (sc0, sc1), dk)
+    front_heads(q8, key, val, ohq, ohk, att, (km, vm), (acc_a, mid), dk)
     pl.semaphore_wait(barrier, len(friends))
     get_wp.wait()
 
@@ -495,6 +500,12 @@
         send(acc_a, r)
 
     loop(blocks, project)
+
+    def turn(r):
+        rows = aligned(r, PAIR)
+        lse[:, rows] = jnp.transpose(dk[rows, :])[: lse.shape[0], :]
+
+    loop(x.shape[0] // PAIR, turn)
 
     get_og.wait()
 
@@ -531,7 +542,8 @@
     get_wc.wait()
 
     def feed(i):
-        j = (i + chunks - 1) % chunks
+        none, one = 1 - (i + chunks - 1) // chunks, 1 - (i + chunks - 2) // chunks
+        j = i - 1 + none + (chunks - 1) * (one - none)
         cols = aligned(j, CHUNK)
 
         def rows_of(r):
@@ -554,8 +566,8 @@
         got = dot_nn(nst[...], hgb[...])
         gf[j, :, :, pl.ds(CHUNK, CHUNK)] = got.reshape(gf.shape[1], gf.shape[2], CHUNK)
         if fuse:
-            pl.when(i == 0)(deep.start)
-            pl.when(i > 0)(lambda: ff.start1(j))
+            pl.when(i == 1)(deep.start)
+            pl.when(i != 1)(lambda: ff.start1(j))
             pl.when(i == 4)(lambda: ff.finish1(0))
         else:
             ff.start1(j)
@@ -605,6 +617,38 @@
 
     loop(blocks, second_back)
     ff.finish2(0)
+
+    def small_copy(i, k, peer, late=1):
+        rows = pl.ds(8 * late, 8)
+        return remote(
+            small.at[k, rows], small_r.at[i, rows], ms.at[4 + 6 * late + i], mr.at[6 * late + i],
+            peer,
+        )
+
+    early, late = slice(0, 8), slice(8, 16)
+    n = chunks * CHUNK // 2
+    small[0, 4:5, :] = sums[0:1, 0:n]
+    small[0, 5:6, :] = sums[0:1, n : 2 * n]
+    small[1, early] = small[0, early]
+
+    def early_one():
+        small_copy(1, 1, peer1, 0).wait()
+        small[2, early] = small[1, early] + small_r[1, early]
+        small_copy(2, 2, peer2, 0).start()
+
+    def early_two():
+        small_copy(2, 2, peer2, 0).wait()
+        small[3, early] = small[2, early] + small_r[2, early]
+        for k in range(3):
+            small_copy(3 + k, 3, peers_z[k], 0).start()
+
+    def early_three():
+        for k in range(3):
+            small_copy(3 + k, 3, peers_z[k], 0).wait()
+        small[4, early] = small[3, early] + (small_r[3, early] + small_r[4, early] + small_r[5, early])
+
+    if fuse:
+        small_copy(1, 1, peer1, 0).start()
     gq[0] = dot_nn(cott[...], att[...].astype(BF16)).reshape(gq.shape[1:])
     pq.start1(0)
 
@@ -674,6 +718,7 @@
                 else:
                     pl.when(p == 0)(deep.finish1)
                     pl.when(p > 0)(lambda: ff.finish3(p - 1))
+                    pl.when(p == pairs - 1)(early_one)
 
         head_back(0)
         head_back(1)
@@ -723,8 +768,8 @@
             rows = pl.ds(pl.multiple_of(r * R + i * SUB, SUB), SUB)
             unit, _ = unit_of(x[rows, :].astype(F32))
             up = acc_a[rows, :]
-            small[0, 6:7, :] = small[0, 6:7, :] + jnp.sum(up * unit, axis=0, keepdims=True)
-            small[0, 7:8, :] = small[0, 7:8, :] + jnp.sum(up, axis=0, keepdims=True)
+            small[0, 8:9, :] = small[0, 8:9, :] + jnp.sum(up * unit, axis=0, keepdims=True)
+            small[0, 9:10, :] = small[0, 9:10, :] + jnp.sum(up, axis=0, keepdims=True)
 
         take_credit(r)
         send(acc_a, r)
@@ -732,26 +777,23 @@
 
     loop(blocks, first_send)
 
-    n = chunks * CHUNK // 2
-    small[0, 4:5, :] = sums[0:1, 0:n]
-    small[0, 5:6, :] = sums[0:1, n : 2 * n]
     m = pairs * PAIR
     for k in range(5):
-        small[0, 8 + k : 9 + k, 0:m] = sums[1 + k : 2 + k, 0:m]
-
-    def small_copy(i, k, peer):
-        return remote(small.at[k], small_r.at[i], ms.at[4 + i], mr.at[i], peer)
-
+        small[0, 10 + k : 11 + k, 0:m] = sums[1 + k : 2 + k, 0:m]
+
+    parts = [(j, k) for j in range(pairs + 1) for k in range(3)]
+    count = len(parts)
     copy = small_copy(0, 0, mate)
     copy.start()
     if fuse:
-        pq.finish1(0)
+        for part in parts[:3]:
+            pq.finish1(*part)
         deep.finish2()
         ff.finish2(4)
         ff.finish3(2)
     copy.wait()
-    line = lax.broadcasted_iota(jnp.int32, small.shape[1:], 0)
-    small[1] = small[0] + jnp.where((line == 6) | (line == 7), small_r[0], 0.0)
+    line = lax.broadcasted_iota(jnp.int32, (8, small.shape[2]), 0)
+    small[1, late] = small[0, late] + jnp.where(line < 2, small_r[0, late], 0.0)
     if fuse:
         small_copy(1, 1, peer1).start()
     last = 4 if fuse else 1
@@ -771,34 +813,41 @@
 
     loop(blocks, first_back)
     if fuse:
-        pq.finish1(1)
-        pq.finish2(0)
-        ff.finish3(3)
-        pq.finish1(2)
-        pq.finish2(1)
-        ff.finish3(4)
-        deep.finish3()
-        pq.finish3(0)
-        pq.finish1(3)
+        early_two()
+        sent = done = 0
+        for i in range(3, count):
+            pq.finish1(*parts[i])
+            while sent < i - 1:
+                pq.finish2(*parts[sent])
+                sent += 1
+            if i == 4:
+                ff.finish3(3)
+            if i == 7:
+                ff.finish3(4)
+                deep.finish3()
+            while done < i - 6:
+                pq.finish3(*parts[done])
+                done += 1
         small_copy(1, 1, peer1).wait()
-        small[2] = small[1] + small_r[1]
+        early_three()
+        small[2, late] = small[1, late] + small_r[1, late]
         small_copy(2, 2, peer2).start()
-        pq.finish2(2)
-        pq.finish3(1)
+        pq.finish2(*parts[count - 2])
         small_copy(2, 2, peer2).wait()
-        small[3] = small[2] + small_r[2]
+        small[3, late] = small[2, late] + small_r[2, late]
         copies = [small_copy(3 + k, 3, peers_z[k]) for k in range(3)]
         for copy in copies:
             copy.start()
-        pq.finish2(3)
-        pq.finish3(2)
+        pq.finish2(*parts[count - 1])
+        for part in parts[done : count - 1]:
+            pq.finish3(*part)
         for copy in copies:
             copy.wait()
-        small[4] = small[3] + (small_r[3] + small_r[4] + small_r[5])
+        small[4, late] = small[3, late] + (small_r[3, late] + small_r[4, late] + small_r[5, late])
     out_small = pltpu.make_async_copy(small.at[last], small_h, lsem.at[0])
     out_small.start()
     if fuse:
-        pq.finish3(3)
+        pq.finish3(*parts[count - 1])
         deep.drain()
         loop(chunks - 1, ff.drain)
     else:
@@ -842,7 +891,7 @@
     DMA = pltpu.SemaphoreType.DMA
     REG = pltpu.SemaphoreType.REGULAR
     blocks = rows // R
-    lines = chunks + pairs + 1
+    lines = chunks + 3 * (pairs + 1)
     recv = (lambda n: V((slots, n, part_rows, 2 * CHUNK), F32)) if fuse else (lambda n: V((1, 1, 8, PAIR), F32))
     scratch = [
         V((rows, heads), F32), V((rows, heads), BF16), V((rows, heads), BF16), V((rows, heads), BF16),
@@ -857,10 +906,9 @@
         V((rows, PAIR), F32), V((rows, PAIR), F32), V((8, hidden), F32),
         V((chunks, *grain, 2 * CHUNK), F32), V((pairs + 1, *grain, 3 * PAIR), F32),
         recv(8), recv(4), recv(3), V((5, 16, width), F32), V((6, 16, width), F32),
-        V((R, rows), F32), V((R, rows), F32),
         DMA((16,)), DMA((blocks,)), DMA((blocks,)), REG((blocks,)),
         DMA((lines,)), DMA((lines,)), DMA((lines,)), DMA((lines,)), DMA((lines,)), DMA((lines,)),
-        REG((4,)), REG((4,)), REG((4,)), DMA((10,)), DMA((6,)), DMA((lines,)), DMA((2,)),
+        REG((4,)), REG((4,)), REG((4,)), DMA((16,)), DMA((12,)), DMA((lines,)), DMA((2,)),
     ]
     return pl.pallas_call(
         partial(main_kernel, fuse, pairs, chunks),
@@ -880,9 +928,12 @@
 def finish_kernel(
     mixed_h, pgrad_h, ff_h, pq_h, small_h,
     mixed_o, pgrad_o, qkv_o, proj_o, expand_o, contract_o,
-    gain_one, shift_one, bias_q, rope, bias_p, gain_two, shift_two, bias_e, bias_c,
-    mixed, pgrad, ff, pq, small, isem, osem,
+    *rest,
 ):
+    tiny_o, (mixed, pgrad, ff, pq, small), tiny, (isem, osem, tsem) = (
+        rest[:9], rest[9:14], rest[14:23], rest[23:],
+    )
+    gain_one, shift_one, bias_q, rope, bias_p, gain_two, shift_two, bias_e, bias_c = tiny
     blocks = mixed.shape[0] // R
     chunks, pairs = ff.shape[0], pq.shape[0] - 1
     jobs = [(small_h, small, [])]
@@ -905,27 +956,31 @@
     gets = [pltpu.make_async_copy(a, b, isem.at[i]) for i, (a, b, _) in enumerate(jobs)]
     for get in gets:
         get.start()
-    puts = []
-    for get, (_, _, todo) in zip(gets, jobs):
-        get.wait()
-        for a, b in todo:
-            puts.append(pltpu.make_async_copy(a, b, osem.at[len(puts)]))
-            puts[-1].start()
+    gets[0].wait()
     heads = bias_q.shape[1]
     for k, out in (
-        (6, gain_one), (7, shift_one), (3, bias_p), (1, gain_two), (2, shift_two), (0, bias_c),
+        (8, gain_one), (9, shift_one), (3, bias_p), (1, gain_two), (2, shift_two), (0, bias_c),
     ):
         out[...] = small[k, :]
     half = bias_e.shape[0] // 2
     bias_e[:half] = small[4, :half]
     bias_e[half:] = small[5, :half]
-    bias_q[...] = small[8:11, :heads]
+    bias_q[...] = small[10:13, :heads]
     for p in range(pairs):
         tile = small[8:16, p * PAIR : (p + 1) * PAIR]
         both = tile + pltpu.roll(tile, PAIR - HALF // 2, 1)
-        rope[2 * p] = both[3:5, : HALF // 2]
-        rope[2 * p + 1] = pltpu.roll(both, HALF, 1)[3:5, : HALF // 2]
-    for put in puts:
+        rope[2 * p] = both[5:7, : HALF // 2]
+        rope[2 * p + 1] = pltpu.roll(both, HALF, 1)[5:7, : HALF // 2]
+    last = [pltpu.make_async_copy(a, b, tsem.at[i]) for i, (a, b) in enumerate(zip(tiny, tiny_o))]
+    for put in last:
+        put.start()
+    puts = []
+    for get, (_, _, todo) in list(zip(gets, jobs))[1:]:
+        get.wait()
+        for a, b in todo:
+            puts.append(pltpu.make_async_copy(a, b, osem.at[len(puts)]))
+            puts[-1].start()
+    for put in puts + last:
         put.wait()
 
 
@@ -941,7 +996,6 @@
         shape(width), shape(hidden), shape(width),
     ]
     any_spec = pl.BlockSpec(memory_space=ANY)
-    vm_spec = pl.BlockSpec(memory_space=pltpu.VMEM)
     reads = 1 + 2 * (rows // R) + ff.shape[0] + pq.shape[0]
     writes = 2 * (rows // R) + 2 * ff.shape[0] + 3 * pq.shape[0] - 2
     big = (mixed, pgrad, ff, pq, small)
@@ -950,9 +1004,9 @@
         name="finish",
         out_shape=outs,
         in_specs=[any_spec] * 5,
-        out_specs=[any_spec] * 6 + [vm_spec] * (len(outs) - 6),
-        scratch_shapes=[pltpu.VMEM(v.shape, v.dtype) for v in big]
-        + [pltpu.SemaphoreType.DMA((reads,)), pltpu.SemaphoreType.DMA((writes,))],
+        out_specs=[any_spec] * len(outs),
+        scratch_shapes=[pltpu.VMEM(v.shape, v.dtype) for v in (*big, *outs[6:])]
+        + [pltpu.SemaphoreType.DMA((n,)) for n in (reads, writes, 9)],
         compiler_params=pltpu.CompilerParams(vmem_limit_bytes=67043328),
     )(*big)
 

time: 171 us -> 160 us (0.936)
  Pallas kernels: 170 us -> 159 us
    pallas_call x1, Pallas kernels: 165 us -> 154 us  [main_call(): pl.pallas_call(partial(main_kernel, fuse, pairs, chunks), name='main', ou...]
where the time goes in v4:
time: 160 us
  Pallas kernels  159 us (99%)
    pallas_call x1, Pallas kernels, main_call(): pl.pallas_call(partial(main_kernel, fuse, pairs, chunks), name='main', ou...  154 us
    pallas_call x1, Pallas kernels, finish(): pl.pallas_call(finish_kernel, name='finish', out_shape=outs, in_specs=[an...  5.1 us

profile of v4, /device:TPU:0, one launch (start us, length us, event | category | flops | bytes accessed | tf_op | source)
XLA Modules:
  0.0 159.9 jit_solution(10451893162136224985)
XLA Ops:
  0.7 154.1 %main.1 = (bf16[1024,768]{1,0:T(8,128)(2,1)}, f32[1024,768]{1,0:T(8,128)}, f32[6,48,512]{2,1,0:T(8,128)}, f32[4,48,384]{2,1,0:T(8,128)}, f32[16,768]{1,0:T(8,128...) custom-call(bf16[1024,768]{1,0:T(8,128)(2,1)} %x_h.1, bf16[1024,768]{1,0:T(8,128)(2,1)} %og_h.1, ...), custom_call_target="tpu_custom_call" | custom-call | tf_op jit(solution)/shard_map/main/pallas_call | solution.py:913
  154.8 5.1 %finish.1 = (bf16[1024,768]{1,0:T(8,128)(2,1)}, f32[1024,768]{1,0:T(8,128)}, f32[3,48,384]{2,1,0:T(8,128)}, f32[48,384]{1,0:T(8,128)}, f32[48,1536]{1,0:T(8,128)...) custom-call(bf16[1024,768]{1,0:T(8,128)(2,1)} %get-tuple-element.35., ...), custom_call_target="tpu_custom_call" | custom-call | tf_op jit(solution)/shard_map/finish/pallas_call | solution.py:1002

commit v5 on v4

--- a/solution.py
+++ b/solution.py
@@ -131,8 +131,8 @@
     loop(rows_all // SUB, norm)
 
     def project(r):
-        rows = aligned(r, R)
-        lane_first = lane_ids(R) % HALF < HALF // 2
+        rows = aligned(r, QR)
+        lane_first = lane_ids(QR) % HALF < HALF // 2
         sign = jnp.where(lane_first, -1.0, 1.0)
         for k, out in ((0, q8), (1, key)):
             got = dot_nn(nf[rows, :], w[:, k * width_all : (k + 1) * width_all]) + b[k : k + 1, :]
@@ -149,10 +149,10 @@
         got = dot_nn(nf[rows, :], w[:, 2 * width_all : 3 * width_all])
         val[rows, :] = (got + b[2:3, :]).astype(BF16)
 
-    loop(rows_all // R, project)
-
-
-def front_heads(q8, key, val, ohq, ohk, att, kxs, scs, lcol):
+    loop(rows_all // QR, project)
+
+
+def front_heads(q8, key, val, ohq, ohk, att, kxs, scs, lcol, after):
     rows_all, width_all = q8.shape
     blocks, pieces_all, wide = rows_all // QR, rows_all // R, scs[0].shape[1] // R
     masks = [head_mask(h).astype(BF16) for h in range(2)]
@@ -161,50 +161,57 @@
         at = (k // wide) * QR
         return scs[h].at[at : at + QR, (k % wide) * R : (k % wide + 1) * R]
 
-    def heads(p):
-        cols = aligned(p, PAIR)
-        for h in range(2):
-            kxs[h][...] = key[:, cols] * masks[h] + ohk[...] * masks[1 - h]
-
-        def scores(h, r):
-            rows = aligned(r, QR)
-            qx = q8[rows, cols] * masks[h] + ohq[rows, :] * masks[1 - h]
-            for k in range(pieces_all):
-                piece(h, k)[...] = dot_nt(qx, kxs[h][k * R : (k + 1) * R, :])
-
-        def weigh(h, r):
-            rows = aligned(r, QR)
-            top = piece(h, 0)[...]
-            for k in range(1, pieces_all):
-                top = jnp.maximum(top, piece(h, k)[...])
-            top = jnp.max(top, axis=-1, keepdims=True)
-            total = jnp.zeros((QR, PAIR), F32)
-            got = jnp.zeros((QR, PAIR), F32)
-            for k in range(pieces_all):
-                grown = jnp.exp(piece(h, k)[...] - top)
-                for m in range(R // PAIR):
-                    total = total + grown[:, m * PAIR : (m + 1) * PAIR]
-                got = got + dot_nn(grown.astype(BF16), val[k * R : (k + 1) * R, cols])
-            total = jnp.sum(total, axis=-1, keepdims=True)
-            got = got * (1.0 / total)
-            lane = lane_ids(QR)
-            if h == 0:
-                att[rows, cols] = got
-            else:
-                att[rows, cols] = jnp.where(lane < HALF, att[rows, cols], got)
-            lcol[rows, :] = jnp.where(lane == p * 2 + h, top + jnp.log(total), lcol[rows, :])
-
-        scores(0, 0)
-
-        def step(r):
-            scores(1, r)
-            weigh(0, r)
-            scores(0, jnp.minimum(r + 1, blocks - 1))
-            weigh(1, r)
-
-        loop(blocks, step)
-
-    loop(width_all // PAIR, heads)
+    pairs = width_all // PAIR
+
+    def keys(h, p):
+        kxs[h][...] = key[:, aligned(p, PAIR)] * masks[h] + ohk[...] * masks[1 - h]
+
+    def scores(h, r, p):
+        rows = aligned(r, QR)
+        qx = q8[rows, aligned(p, PAIR)] * masks[h] + ohq[rows, :] * masks[1 - h]
+        for k in range(pieces_all):
+            piece(h, k)[...] = dot_nt(qx, kxs[h][k * R : (k + 1) * R, :])
+
+    def weigh(h, r, p):
+        rows, cols = aligned(r, QR), aligned(p, PAIR)
+        top = piece(h, 0)[...]
+        for k in range(1, pieces_all):
+            top = jnp.maximum(top, piece(h, k)[...])
+        top = jnp.max(top, axis=-1, keepdims=True)
+        total = jnp.zeros((QR, PAIR), F32)
+        got = jnp.zeros((QR, PAIR), F32)
+        for k in range(pieces_all):
+            grown = jnp.exp(piece(h, k)[...] - top)
+            for m in range(R // PAIR):
+                total = total + grown[:, m * PAIR : (m + 1) * PAIR]
+            got = got + dot_nn(grown.astype(BF16), val[k * R : (k + 1) * R, cols])
+        total = jnp.sum(total, axis=-1, keepdims=True)
+        got = got * (1.0 / total)
+        lane = lane_ids(QR)
+        if h == 0:
+            att[rows, cols] = got
+        else:
+            att[rows, cols] = jnp.where(lane < HALF, att[rows, cols], got)
+        lcol[rows, :] = jnp.where(lane == p * 2 + h, top + jnp.log(total), lcol[rows, :])
+
+    keys(0, 0)
+    keys(1, 0)
+    scores(0, 0, 0)
+
+    def half(r):
+        def step(p):
+            n = jnp.minimum(r * pairs + p + 1, blocks * pairs - 1)
+            scores(1, r, p)
+            weigh(0, r, p)
+            keys(0, n % pairs)
+            scores(0, n // pairs, n % pairs)
+            weigh(1, r, p)
+            keys(1, n % pairs)
+
+        loop(pairs, step)
+        after(r)
+
+    loop(blocks, half)
 
 
 PARTS = 16
@@ -222,7 +229,7 @@
     acc_a, acc_b, xbuf, mid, cott, ns, nst, act, hgb, dgrad, delta,
     km, vm, kt, kmt, dk, dv, dqt, qkvg, cos, sin, sums,
     gf, gq, r1, r2, r3, small, small_r,
-    lsem, xs, xr, credit, s1, e1, s2, e2, s3, e3, c1, c2, c3, ms, mr, osem, zs,
+    lsem, xs, xr, credit, s1, e1, s2, e2, s3, e3, c1, c2, c3, ms, mr, osem, zs, s4, e4,
     ) = rest
     gain_one, shift_one, bias_p, gain_two, shift_two, bias_e, bias_c = (
         v[...].reshape(1, -1)
@@ -240,6 +247,9 @@
         peer1 = (me + (1 - 2 * fst) * (1 + core), core)
         peer2 = (me + (1 - 2 * snd) * (2 - core), core)
         peers_z = [(((zz + j) % 4) * 4 + me % 4, core) for j in (1, 2, 3)]
+        odd, across = zz % 2, (zz + 2) % 4
+        near = ((zz + 1 - 2 * odd) * 4 + me % 4, core)
+        far = (across * 4 + me % 4, core)
 
         def where(z, f, s):
             return z * 4 + s * (2 - core) + f * (1 + core)
@@ -381,31 +391,63 @@
                 self.whole(j, k, 3, s3, e3, r3, peers_z[0]).wait_send()
                 self.result(j, k).wait()
 
+    class Two(Line):
+        def finish2(self, j, k=0):
+            self.whole(j, k, 4, s2, e2, r2, peer2).wait_recv()
+            c = self.cols(k)
+
+            def one(i):
+                self.add(j, k, where(i, fst, snd), r2[j, i, :, c])
+
+            loop(4, one)
+            self.give(c2, j, [peer2])
+            for m in range(2):
+                b = where(1 - odd + 2 * m, fst, snd)
+                self.step(j, k, r3, b, m, s3, e3, near).start()
+
+        def finish3(self, j, k=0):
+            self.whole(j, k, 2, s3, e3, r3, near).wait_recv()
+            c = self.cols(k)
+            for m in range(2):
+                self.add(j, k, where(odd + 2 * m, fst, snd), r3[j, m, :, c])
+            self.step(j, k, r3, where(across, fst, snd), 2, s4, e4, far).start()
+
+        def finish4(self, j, k=0):
+            self.step(j, k, r3, 0, 2, s4, e4, far).wait_recv()
+            self.add(j, k, me, r3[j, 2, :, self.cols(k)])
+            self.give(c3, j, peers_z)
+            self.result(j, k).start()
+
+        def drain(self, j):
+            for k in range(self.parts):
+                self.whole(j, k, 8, s1, e1, r1, peer1).wait_send()
+                self.whole(j, k, 4, s2, e2, r2, peer2).wait_send()
+                self.whole(j, k, 2, s3, e3, r3, near).wait_send()
+                self.step(j, k, r3, 0, 2, s4, e4, far).wait_send()
+                self.result(j, k).wait()
+
     class Deep:
-        def __init__(self, grads, j, out):
-            self.g, self.j, self.out = grads, j, out
-
-        def quarter(self, k):
+        def __init__(self, grads, j, out, line):
+            self.g, self.j, self.out, self.line = grads, j, out, line
+
+        def one(self):
             j = self.j
-            src = self.g.at[j, pl.ds(((zz + k + 1) % 4) * 4, 4)]
-            if k < 2:
-                return remote(src, r1.at[j, pl.ds(4 * k, 4)], s1.at[j], e1.at[j], peers_z[k])
-            return remote(src, r2.at[j], s2.at[j], e2.at[j], peers_z[k])
+            return remote(self.g.at[j, pl.ds(0, 8)], r1.at[j], s1.at[j], e1.at[j], near)
 
         def two(self):
             j = self.j
-            return remote(self.g.at[j, pl.ds(0, 8)], r1.at[j], s1.at[j], e1.at[j], peers_z[0])
-
-        def halves(self):
+            return remote(self.g.at[j, pl.ds(across * 4, 4)], r2.at[j], s2.at[j], e2.at[j], far)
+
+        def three(self):
             j = self.j
             return remote(
                 self.g.at[j, pl.ds(0, 2)], r3.at[j, pl.ds(0, 2)], s3.at[j], e3.at[j], peer1
             )
 
-        def last(self):
+        def four(self):
             return remote(
-                self.g.at[self.j, where(zz, fst, 1 - snd)], r3.at[self.j, 2], zs.at[0], zs.at[1],
-                peer2,
+                self.g.at[self.j, where(zz, fst, 1 - snd)], r3.at[self.j, 2],
+                zs.at[2 * self.line], zs.at[2 * self.line + 1], peer2,
             )
 
         def result(self):
@@ -414,42 +456,53 @@
             )
 
         def start(self):
-            for k in range(3):
-                self.quarter(k).start()
+            j = self.j
+            for m in range(2):
+                remote(
+                    self.g.at[j, pl.ds((1 - odd + 2 * m) * 4, 4)], r1.at[j, pl.ds(4 * m, 4)],
+                    s1.at[j], e1.at[j], near,
+                ).start()
 
         def finish1(self):
             j = self.j
+            self.one().wait_recv()
+
+            def add(i):
+                b = (odd + 2 * (i // 4)) * 4 + i % 4
+                self.g[j, b] = self.g[j, b] + r1[j, i]
+
+            loop(8, add)
+            self.two().start()
+
+        def finish2(self):
+            j = self.j
             self.two().wait_recv()
-            self.quarter(2).wait_recv()
-
-            def one(i):
-                b = zz * 4 + i
-                self.g[j, b] = self.g[j, b] + r1[j, i] + r1[j, 4 + i] + r2[j, i]
-
-            loop(4, one)
+
+            def add(i):
+                self.g[j, zz * 4 + i] = self.g[j, zz * 4 + i] + r2[j, i]
+
+            loop(4, add)
             for s in range(2):
                 remote(
                     self.g.at[j, where(zz, 1 - fst, s)], r3.at[j, s], s3.at[j], e3.at[j], peer1
                 ).start()
 
-        def finish2(self):
+        def finish3(self):
             j = self.j
-            self.halves().wait_recv()
+            self.three().wait_recv()
             for s in range(2):
                 b = where(zz, fst, s)
                 self.g[j, b] = self.g[j, b] + r3[j, s]
-            self.last().start()
-
-        def finish3(self):
-            self.last().wait_recv()
+            self.four().start()
+
+        def finish4(self):
+            self.four().wait_recv()
             self.g[self.j, me] = self.g[self.j, me] + r3[self.j, 2]
             self.result().start()
 
         def drain(self):
-            self.two().wait_send()
-            self.quarter(2).wait_send()
-            self.halves().wait_send()
-            self.last().wait_send()
+            for copy in (self.one(), self.two(), self.three(), self.four()):
+                copy.wait_send()
             self.result().wait()
 
     class Plain:
@@ -471,9 +524,9 @@
             self.copy(j).wait()
 
     kind = Line if fuse else Plain
-    ff = kind(gf, 0, 2 * CHUNK, ff_h, "give", 1)
+    ff = (Two if fuse else Plain)(gf, 0, 2 * CHUNK, ff_h, "give", 1)
     pq = kind(gq, chunks, 3 * PAIR, pq_h, "take", 3)
-    deep = Deep(gf, chunks - 1, ff_h)
+    deep = [Deep(gf, chunks - 1 - n, ff_h, n) for n in range(2)]
 
     small[...] = jnp.zeros_like(small)
     sums[...] = jnp.zeros_like(sums)
@@ -484,22 +537,24 @@
         lines = [freqs[n, axis : axis + 1, :] for n in range(heads // HALF) for _ in range(2)]
         turns.append(jnp.concatenate(lines, axis=1))
     front_place(grids, slots, turns, ohq, ohk, acc_b, pos)
+    put_cossin = load(acc_b.at[:, pl.ds(0, 2 * heads)], cossin_h, 11)
     get_x.wait()
     for copy in get_wq:
         copy.wait()
     front_rows(x, gain_one, shift_one, we, bias_q, q8, key, val, ns, acc_b)
     get_we = load(we_h, we, 5)
     put_nf = load(ns, nf_h, 10)
-    put_cossin = load(acc_b.at[:, pl.ds(0, 2 * heads)], cossin_h, 11)
-    front_heads(q8, key, val, ohq, ohk, att, (km, vm), (acc_a, mid), dk)
+    put_cossin.wait()
+    get_wp.wait()
     pl.semaphore_wait(barrier, len(friends))
-    get_wp.wait()
 
     def project(r):
-        acc_a[aligned(r, R), :] = dot_nn(att[aligned(r, R), :].astype(BF16), wp[...])
-        send(acc_a, r)
-
-    loop(blocks, project)
+        for n in range(QR // R):
+            rows = aligned(r * (QR // R) + n, R)
+            acc_a[rows, :] = dot_nn(att[rows, :].astype(BF16), wp[...])
+            send(acc_a, r * (QR // R) + n)
+
+    front_heads(q8, key, val, ohq, ohk, att, (km, vm), (mid, acc_b), dk, project)
 
     def turn(r):
         rows = aligned(r, PAIR)
@@ -519,7 +574,6 @@
 
     loop(blocks, mask_cot)
     put_nf.wait()
-    put_cossin.wait()
 
     def second_norm(r):
         exchange(acc_a, r).wait()
@@ -542,12 +596,12 @@
     get_wc.wait()
 
     def feed(i):
-        none, one = 1 - (i + chunks - 1) // chunks, 1 - (i + chunks - 2) // chunks
-        j = i - 1 + none + (chunks - 1) * (one - none)
+        none, upto = 1 - (i + chunks - 1) // chunks, 1 - (i + chunks - 3) // chunks
+        j = (i - 2) * (1 - upto) + (chunks - i) * (upto - none)
         cols = aligned(j, CHUNK)
 
         def rows_of(r):
-            rows = aligned(r, R)
+            rows = aligned(r, QR)
             hidden = dot_nn(ns[rows, :], we[:, cols]) + sums[7:8, cols]
             upstream = dot_nt(cot[rows, :], wc[cols, :])
             phi = 0.5 * (1.0 + lax.erf(hidden * (0.5**0.5)))
@@ -560,27 +614,42 @@
             acc_b[rows, :] = acc_b[rows, :] + dot_nn(active, wc[cols, :])
             acc_a[rows, :] = acc_a[rows, :] + dot_nt(hgrad, we[:, cols])
 
-        loop(blocks, rows_of)
+            def leave():
+                for n in range(QR // R):
+                    take_credit(r * (QR // R) + n)
+                    send(acc_a, r * (QR // R) + n)
+
+            pl.when(i == chunks - 1)(leave)
+
+        loop(x.shape[0] // QR, rows_of)
         got = dot_nn(cott[...], act[...])
         gf[j, :, :, pl.ds(0, CHUNK)] = got.reshape(gf.shape[1], gf.shape[2], CHUNK)
         got = dot_nn(nst[...], hgb[...])
         gf[j, :, :, pl.ds(CHUNK, CHUNK)] = got.reshape(gf.shape[1], gf.shape[2], CHUNK)
         if fuse:
-            pl.when(i == 1)(deep.start)
-            pl.when(i != 1)(lambda: ff.start1(j))
+            pl.when(i == 1)(deep[0].start)
+            pl.when(i == 2)(deep[1].start)
+            pl.when((i != 1) & (i != 2))(lambda: ff.start1(j))
             pl.when(i == 4)(lambda: ff.finish1(0))
         else:
             ff.start1(j)
 
     loop(chunks, feed)
 
-    def send_second(r):
-        take_credit(r)
-        send(acc_a, r)
-
-    loop(blocks, send_second)
     get_nf = load(nf_h, ns, 0)
-    ff.finish1(1)
+    get_wq = [
+        load(wq_h.at[k], we.at[:, pl.ds(k * pairs * PAIR, pairs * PAIR)], 4 + k) for k in range(3)
+    ]
+    kt[...] = jnp.transpose(key[...])
+    get_nf.wait()
+
+    def turn_first(r):
+        nst[:, aligned(r, R)] = jnp.transpose(ns[aligned(r, R), :])
+
+    loop(blocks, turn_first)
+    if fuse:
+        deep[0].finish1()
+        ff.finish1(1)
 
     def second_back(r):
         exchange(acc_a, r).wait()
@@ -598,7 +667,6 @@
             small[0, 3:4, :] = small[0, 3:4, :] + jnp.sum(
                 low.astype(F32), axis=0, keepdims=True
             )
-            acc_a[rows, :] = jnp.zeros_like(up)
 
         loop(R // SUB, sub)
         give_credit(r)
@@ -616,7 +684,8 @@
         )
 
     loop(blocks, second_back)
-    ff.finish2(0)
+    if fuse:
+        ff.finish2(0)
 
     def small_copy(i, k, peer, late=1):
         rows = pl.ds(8 * late, 8)
@@ -651,23 +720,14 @@
         small_copy(1, 1, peer1, 0).start()
     gq[0] = dot_nn(cott[...], att[...].astype(BF16)).reshape(gq.shape[1:])
     pq.start1(0)
+    if fuse:
+        ff.finish1(2)
 
     def send_mixed(r):
         take_credit(r)
         send(acc_b, r)
 
     loop(blocks, send_mixed)
-
-    get_nf.wait()
-
-    def turn_first(r):
-        nst[:, aligned(r, R)] = jnp.transpose(ns[aligned(r, R), :])
-
-    loop(blocks, turn_first)
-    get_wq = [
-        load(wq_h.at[k], we.at[:, pl.ds(k * pairs * PAIR, pairs * PAIR)], 4 + k) for k in range(3)
-    ]
-    kt[...] = jnp.transpose(key[...])
 
     def mixed_block(r):
         exchange(acc_b, r).wait()
@@ -676,9 +736,37 @@
         give_credit(r)
         pltpu.make_async_copy(ns.at[rows, :], mixed_h.at[rows, :], ms.at[r]).start()
 
-    loop(blocks, mixed_block)
-    for copy in get_wq:
-        copy.wait()
+    def thrice(step, j):
+        for k in range(3):
+            step(j, k)
+
+    def gap0():
+        ff.finish2(1)
+
+    def gap1():
+        deep[1].finish1()
+        ff.finish1(3)
+
+    def gap2():
+        deep[0].finish2()
+        ff.finish3(0)
+        ff.finish2(2)
+
+    def gap3():
+        ff.finish3(1)
+        thrice(pq.finish1, 0)
+
+    def gap4():
+        deep[1].finish2()
+        ff.finish2(3)
+        ff.finish4(0)
+
+    def gap5():
+        early_one()
+        thrice(pq.finish2, 0)
+        thrice(pq.finish1, 1)
+
+    between = (gap0, gap1, gap2, gap3, gap4, gap5)
 
     def pair_back(p):
         cols = aligned(p, PAIR)
@@ -712,13 +800,8 @@
 
             loop(blocks, query_back)
             if fuse:
-                if h == 0:
-                    ff.finish1(p + 2)
-                    ff.finish2(p + 1)
-                else:
-                    pl.when(p == 0)(deep.finish1)
-                    pl.when(p > 0)(lambda: ff.finish3(p - 1))
-                    pl.when(p == pairs - 1)(early_one)
+                for q in range(3):
+                    pl.when(p == q)(lambda q=q: between[2 * q + h]())
 
         head_back(0)
         head_back(1)
@@ -744,7 +827,7 @@
                 grads.append((grad * c + swapped * s).astype(BF16))
             grads.append(dv[rows, :].astype(BF16))
             for k, low in enumerate(grads):
-                qkvg[rows, k * PAIR : (k + 1) * PAIR] = low
+                qkvg[p, rows, k * PAIR : (k + 1) * PAIR] = low
                 sums[k + 1 : k + 2, cols] = sums[k + 1 : k + 2, cols] + jnp.sum(
                     low.astype(F32), axis=0, keepdims=True
                 )
@@ -752,13 +835,9 @@
                 sums[k + 4 : k + 5, cols] = sums[k + 4 : k + 5, cols] + jnp.sum(
                     total * pos[rows, k + 1 : k + 2], axis=0, keepdims=True
                 )
-            weight = jnp.concatenate(
-                [we[:, aligned(k * pairs + p, PAIR)] for k in range(3)], axis=1
-            )
-            acc_a[rows, :] = acc_a[rows, :] + dot_nt(qkvg[rows, :], weight)
 
         loop(blocks, turn_back)
-        gq[p + 1] = dot_nn(nst[...], qkvg[...]).reshape(gq.shape[1:])
+        gq[p + 1] = dot_nn(nst[...], qkvg[p]).reshape(gq.shape[1:])
         pq.start1(p + 1)
 
     loop(pairs, pair_back)
@@ -771,31 +850,46 @@
             small[0, 8:9, :] = small[0, 8:9, :] + jnp.sum(up * unit, axis=0, keepdims=True)
             small[0, 9:10, :] = small[0, 9:10, :] + jnp.sum(up, axis=0, keepdims=True)
 
+        rows = aligned(r, R)
+        total = jnp.zeros((R, acc_a.shape[1]), F32)
+        for p in range(pairs):
+            weight = jnp.concatenate(
+                [we[:, (k * pairs + p) * PAIR : (k * pairs + p + 1) * PAIR] for k in range(3)],
+                axis=1,
+            )
+            total = total + dot_nt(qkvg[p, rows, :], weight)
+        acc_a[rows, :] = total
         take_credit(r)
         send(acc_a, r)
         loop(R // SUB, sub)
 
+    if fuse:
+        deep[0].finish3()
+        ff.finish3(2)
+        ff.finish4(1)
+        thrice(pq.finish2, 1)
+    loop(blocks, mixed_block)
+    for copy in get_wq:
+        copy.wait()
     loop(blocks, first_send)
 
     m = pairs * PAIR
     for k in range(5):
         small[0, 10 + k : 11 + k, 0:m] = sums[1 + k : 2 + k, 0:m]
 
-    parts = [(j, k) for j in range(pairs + 1) for k in range(3)]
-    count = len(parts)
     copy = small_copy(0, 0, mate)
     copy.start()
     if fuse:
-        for part in parts[:3]:
-            pq.finish1(*part)
-        deep.finish2()
-        ff.finish2(4)
-        ff.finish3(2)
+        thrice(pq.finish1, 2)
+        deep[1].finish3()
+        ff.finish3(3)
+        ff.finish4(2)
     copy.wait()
     line = lax.broadcasted_iota(jnp.int32, (8, small.shape[2]), 0)
     small[1, late] = small[0, late] + jnp.where(line < 2, small_r[0, late], 0.0)
     if fuse:
         small_copy(1, 1, peer1).start()
+        thrice(pq.finish2, 2)
     last = 4 if fuse else 1
 
     def first_back(r):
@@ -814,42 +908,37 @@
     loop(blocks, first_back)
     if fuse:
         early_two()
-        sent = done = 0
-        for i in range(3, count):
-            pq.finish1(*parts[i])
-            while sent < i - 1:
-                pq.finish2(*parts[sent])
-                sent += 1
-            if i == 4:
-                ff.finish3(3)
-            if i == 7:
-                ff.finish3(4)
-                deep.finish3()
-            while done < i - 6:
-                pq.finish3(*parts[done])
-                done += 1
+        ff.finish4(3)
+        thrice(pq.finish3, 0)
+        pq.finish1(3, 0)
+        pq.finish1(3, 1)
+        pq.finish2(3, 0)
+        thrice(pq.finish3, 1)
+        pq.finish1(3, 2)
         small_copy(1, 1, peer1).wait()
-        early_three()
         small[2, late] = small[1, late] + small_r[1, late]
         small_copy(2, 2, peer2).start()
-        pq.finish2(*parts[count - 2])
+        pq.finish2(3, 1)
+        pq.finish2(3, 2)
+        deep[0].finish4()
+        deep[1].finish4()
+        early_three()
         small_copy(2, 2, peer2).wait()
         small[3, late] = small[2, late] + small_r[2, late]
         copies = [small_copy(3 + k, 3, peers_z[k]) for k in range(3)]
         for copy in copies:
             copy.start()
-        pq.finish2(*parts[count - 1])
-        for part in parts[done : count - 1]:
-            pq.finish3(*part)
+        thrice(pq.finish3, 2)
+        thrice(pq.finish3, 3)
         for copy in copies:
             copy.wait()
         small[4, late] = small[3, late] + (small_r[3, late] + small_r[4, late] + small_r[5, late])
     out_small = pltpu.make_async_copy(small.at[last], small_h, lsem.at[0])
     out_small.start()
     if fuse:
-        pq.finish3(*parts[count - 1])
-        deep.drain()
-        loop(chunks - 1, ff.drain)
+        deep[0].drain()
+        deep[1].drain()
+        loop(chunks - 2, ff.drain)
     else:
         loop(chunks, ff.drain)
     loop(pairs + 1, pq.drain)
@@ -902,13 +991,13 @@
         V((width, rows), BF16), V((rows, width), BF16), V((width, rows), BF16),
         V((rows, CHUNK), BF16), V((rows, CHUNK), BF16), V((rows, heads), BF16), V((8, rows), F32),
         V((rows, PAIR), BF16), V((rows, PAIR), BF16), V((heads, rows), BF16), V((PAIR, rows), BF16),
-        V((rows, PAIR), F32), V((rows, PAIR), F32), V((PAIR, rows), F32), V((rows, 3 * PAIR), BF16),
+        V((rows, PAIR), F32), V((rows, PAIR), F32), V((PAIR, rows), F32), V((pairs, rows, 3 * PAIR), BF16),
         V((rows, PAIR), F32), V((rows, PAIR), F32), V((8, hidden), F32),
         V((chunks, *grain, 2 * CHUNK), F32), V((pairs + 1, *grain, 3 * PAIR), F32),
         recv(8), recv(4), recv(3), V((5, 16, width), F32), V((6, 16, width), F32),
         DMA((16,)), DMA((blocks,)), DMA((blocks,)), REG((blocks,)),
         DMA((lines,)), DMA((lines,)), DMA((lines,)), DMA((lines,)), DMA((lines,)), DMA((lines,)),
-        REG((4,)), REG((4,)), REG((4,)), DMA((16,)), DMA((12,)), DMA((lines,)), DMA((2,)),
+        REG((4,)), REG((4,)), REG((4,)), DMA((16,)), DMA((12,)), DMA((lines,)), DMA((4,)), DMA((chunks,)), DMA((chunks,)),
     ]
     return pl.pallas_call(
         partial(main_kernel, fuse, pairs, chunks),

time: 160 us -> 158 us (0.988)
  Pallas kernels: 159 us -> 157 us
    pallas_call x1, Pallas kernels: 154 us -> 152 us  [main_call(): pl.pallas_call(partial(main_kernel, fuse, pairs, chunks), name='main', ou...]
where the time goes in v5:
time: 158 us
  Pallas kernels  157 us (99%)
    pallas_call x1, Pallas kernels, main_call(): pl.pallas_call(partial(main_kernel, fuse, pairs, chunks), name='main', ou...  152 us
    pallas_call x1, Pallas kernels, finish(): pl.pallas_call(finish_kernel, name='finish', out_shape=outs, in_specs=[an...  5.1 us

profile of v5, /device:TPU:0, one launch (start us, length us, event | category | flops | bytes accessed | tf_op | source)
XLA Modules:
  0.0 158.1 jit_solution(10094686108876738475)
XLA Ops:
  0.7 152.4 %main.1 = (bf16[1024,768]{1,0:T(8,128)(2,1)}, f32[1024,768]{1,0:T(8,128)}, f32[6,48,512]{2,1,0:T(8,128)}, f32[4,48,384]{2,1,0:T(8,128)}, f32[16,768]{1,0:T(8,128...) custom-call(bf16[1024,768]{1,0:T(8,128)(2,1)} %x_h.1, bf16[1024,768]{1,0:T(8,128)(2,1)} %og_h.1, ...), custom_call_target="tpu_custom_call" | custom-call | tf_op jit(solution)/shard_map/main/pallas_call | solution.py:1002
  153.0 5.1 %finish.1 = (bf16[1024,768]{1,0:T(8,128)(2,1)}, f32[1024,768]{1,0:T(8,128)}, f32[3,48,384]{2,1,0:T(8,128)}, f32[48,384]{1,0:T(8,128)}, f32[48,1536]{1,0:T(8,128)...) custom-call(bf16[1024,768]{1,0:T(8,128)(2,1)} %get-tuple-element.35., ...), custom_call_target="tpu_custom_call" | custom-call | tf_op jit(solution)/shard_map/finish/pallas_call | solution.py:1091

commit v6 on v5

--- a/solution.py
+++ b/solution.py
@@ -635,6 +635,9 @@
             ff.start1(j)
 
     loop(chunks, feed)
+    if fuse:
+        deep[0].finish1()
+        ff.finish1(1)
 
     get_nf = load(nf_h, ns, 0)
     get_wq = [
@@ -647,9 +650,6 @@
         nst[:, aligned(r, R)] = jnp.transpose(ns[aligned(r, R), :])
 
     loop(blocks, turn_first)
-    if fuse:
-        deep[0].finish1()
-        ff.finish1(1)
 
     def second_back(r):
         exchange(acc_a, r).wait()
@@ -753,8 +753,8 @@
         ff.finish2(2)
 
     def gap3():
+        thrice(pq.finish1, 0)
         ff.finish3(1)
-        thrice(pq.finish1, 0)
 
     def gap4():
         deep[1].finish2()
@@ -762,9 +762,9 @@
         ff.finish4(0)
 
     def gap5():
-        early_one()
         thrice(pq.finish2, 0)
         thrice(pq.finish1, 1)
+        early_one()
 
     between = (gap0, gap1, gap2, gap3, gap4, gap5)
 
@@ -864,10 +864,11 @@
         loop(R // SUB, sub)
 
     if fuse:
-        deep[0].finish3()
         ff.finish3(2)
         ff.finish4(1)
         thrice(pq.finish2, 1)
+        deep[0].finish3()
+        pq.finish1(2, 0)
     loop(blocks, mixed_block)
     for copy in get_wq:
         copy.wait()
@@ -880,7 +881,8 @@
     copy = small_copy(0, 0, mate)
     copy.start()
     if fuse:
-        thrice(pq.finish1, 2)
+        pq.finish1(2, 1)
+        pq.finish1(2, 2)
         deep[1].finish3()
         ff.finish3(3)
         ff.finish4(2)
@@ -905,7 +907,6 @@
         rows = aligned(r, R)
         pltpu.make_async_copy(mid.at[rows, :], pgrad_h.at[rows, :], xs.at[r]).start()
 
-    loop(blocks, first_back)
     if fuse:
         early_two()
         ff.finish4(3)
@@ -928,11 +929,14 @@
         copies = [small_copy(3 + k, 3, peers_z[k]) for k in range(3)]
         for copy in copies:
             copy.start()
+        loop(blocks, first_back)
         thrice(pq.finish3, 2)
         thrice(pq.finish3, 3)
         for copy in copies:
             copy.wait()
         small[4, late] = small[3, late] + (small_r[3, late] + small_r[4, late] + small_r[5, late])
+    if not fuse:
+        loop(blocks, first_back)
     out_small = pltpu.make_async_copy(small.at[last], small_h, lsem.at[0])
     out_small.start()
     if fuse:

time: 158 us -> 157 us (level)
  no operation moved by 1% of the time
where the time goes in v6:
time: 157 us
  Pallas kernels  156 us (99%)
    pallas_call x1, Pallas kernels, main_call(): pl.pallas_call(partial(main_kernel, fuse, pairs, chunks), name='main', ou...  151 us
    pallas_call x1, Pallas kernels, finish(): pl.pallas_call(finish_kernel, name='finish', out_shape=outs, in_specs=[an...  5.1 us

profile of v6, /device:TPU:0, one launch (start us, length us, event | category | flops | bytes accessed | tf_op | source)
XLA Modules:
  0.0 156.8 jit_solution(12618790489325666812)
XLA Ops:
  0.7 151.1 %main.1 = (bf16[1024,768]{1,0:T(8,128)(2,1)}, f32[1024,768]{1,0:T(8,128)}, f32[6,48,512]{2,1,0:T(8,128)}, f32[4,48,384]{2,1,0:T(8,128)}, f32[16,768]{1,0:T(8,128...) custom-call(bf16[1024,768]{1,0:T(8,128)(2,1)} %x_h.1, bf16[1024,768]{1,0:T(8,128)(2,1)} %og_h.1, ...), custom_call_target="tpu_custom_call" | custom-call | tf_op jit(solution)/shard_map/main/pallas_call | solution.py:1006
  151.7 5.1 %finish.1 = (bf16[1024,768]{1,0:T(8,128)(2,1)}, f32[1024,768]{1,0:T(8,128)}, f32[3,48,384]{2,1,0:T(8,128)}, f32[48,384]{1,0:T(8,128)}, f32[48,1536]{1,0:T(8,128)...) custom-call(bf16[1024,768]{1,0:T(8,128)(2,1)} %get-tuple-element.35., ...), custom_call_target="tpu_custom_call" | custom-call | tf_op jit(solution)/shard_map/finish/pallas_call | solution.py:1095

commit v7 on v6

--- a/solution.py
+++ b/solution.py
@@ -757,9 +757,9 @@
         ff.finish3(1)
 
     def gap4():
-        deep[1].finish2()
         ff.finish2(3)
         ff.finish4(0)
+        deep[1].finish2()
 
     def gap5():
         thrice(pq.finish2, 0)

time: 157 us -> 157 us (level)
  no operation moved by 1% of the time
where the time goes in v7:
time: 157 us
  Pallas kernels  156 us (99%)
    pallas_call x1, Pallas kernels, main_call(): pl.pallas_call(partial(main_kernel, fuse, pairs, chunks), name='main', ou...  151 us
    pallas_call x1, Pallas kernels, finish(): pl.pallas_call(finish_kernel, name='finish', out_shape=outs, in_specs=[an...  5.1 us

profile of v7, /device:TPU:0, one launch (start us, length us, event | category | flops | bytes accessed | tf_op | source)
XLA Modules:
  0.0 156.7 jit_solution(6918396690669751182)
XLA Ops:
  0.7 151.0 %main.1 = (bf16[1024,768]{1,0:T(8,128)(2,1)}, f32[1024,768]{1,0:T(8,128)}, f32[6,48,512]{2,1,0:T(8,128)}, f32[4,48,384]{2,1,0:T(8,128)}, f32[16,768]{1,0:T(8,128...) custom-call(bf16[1024,768]{1,0:T(8,128)(2,1)} %x_h.1, bf16[1024,768]{1,0:T(8,128)(2,1)} %og_h.1, ...), custom_call_target="tpu_custom_call" | custom-call | tf_op jit(solution)/shard_map/main/pallas_call | solution.py:1006
  151.6 5.1 %finish.1 = (bf16[1024,768]{1,0:T(8,128)(2,1)}, f32[1024,768]{1,0:T(8,128)}, f32[3,48,384]{2,1,0:T(8,128)}, f32[48,384]{1,0:T(8,128)}, f32[48,1536]{1,0:T(8,128)...) custom-call(bf16[1024,768]{1,0:T(8,128)(2,1)} %get-tuple-element.35., ...), custom_call_target="tpu_custom_call" | custom-call | tf_op jit(solution)/shard_map/finish/pallas_call | solution.py:1095
